TPU v7x, 32 devices: a whole 2x2x4 slice. The times are simulated.
32 devices in a mesh: row: 8 (over y, x, core), col: 4 (over z).
Axes of the slice: x: 2, y: 2, z: 4, core: 2. Of those that a mesh axis runs over, the one named last changes fastest.
Arguments:
- in_map: bfloat16 [128, 128, 256], P('row', 'col'), may hold values from -6 to 6
- tile_w: bfloat16 [3, 3, 256, 256], replicated, may hold values from -0.125 to 0.125
- head_w1: bfloat16 [3, 3, 256, 256], replicated, may hold values from -0.125 to 0.125
- head_w2: bfloat16 [3, 3, 256, 256], replicated, may hold values from -0.125 to 0.125
- box_row: int32 [64, 4], P('row', 'col'), may hold values from 0 to 2
- box_col: int32 [64, 4], P('row', 'col'), may hold values from 0 to 18
- box_target: int32 [64, 4], P('row', 'col'), may hold values from -1 to 15, as said below
- head_cot: bfloat16 [32, 4, 14, 14, 256], P('row', 'col'), may hold values from -6 to 6
Outputs:
- grad_map: bfloat16 [128, 128, 256], P('row', 'col')
- grad_w1: float32 [3, 3, 256, 256], replicated
- grad_w2: float32 [3, 3, 256, 256], replicated
Inputs may be any that keep to these rules, and one draw needn't show every extreme that they name: `box_target`: within each row r of tiles, every head slot d * 4 + h (d below 4, h below 4) is named by exactly one tile slot, and empty slots hold -1. A tile names at most 2 head slots of one device, so it holds at most 8 boxes; in every row of tiles one tile holds 8 boxes, 2 for each device of the row.
All inputs are finite; a program needn't handle non-finite values.
Results may differ from a plain program's by a relative error of at most 0.012.
Values may be sent and summed in bfloat16 or wider, within the bound.
No kernel may reach another device: no remote copies, remote signals or barrier semaphores. Data moves between devices by JAX's collectives and lax.ppermute only.
A program may use at most 64 MiB of HBM per device.

v0:
```python
import math

import jax
import jax.numpy as jnp
from jax import lax
from jax.sharding import PartitionSpec as P

LAYOUT = ("NHWC", "HWIO", "NHWC")


def padded_2(shard, sides, width):
    for axis, dim in sides:
        size, length = (lax.axis_size(axis), shard.shape[dim])
        up = [(i, (i + 1) % size) for i in range(size - 1)]
        down = [(j, i) for i, j in up]
        last = lax.slice_in_dim(shard, length - width, length, axis=dim)
        leading = lax.slice_in_dim(shard, 0, width, axis=dim)
        before = lax.ppermute(last, axis, up)
        after = lax.ppermute(leading, axis, down)
        shard = jnp.concatenate([before, shard, after], axis=dim)
    return shard


def conv_pad(inputs, kernel, margin):
    return lax.conv_general_dilated(
        inputs,
        kernel,
        (1, 1),
        ((margin, margin), (margin, margin)),
        dimension_numbers=LAYOUT,
        preferred_element_type=jnp.float32,
    )


def flip_weights(kernel):
    return jnp.transpose(jnp.flip(kernel, (0, 1)), (0, 1, 3, 2))


def silu_slope(values):
    sigma = jax.nn.sigmoid(values)
    return sigma * (1.0 + values * (1.0 - sigma))


def weight_grad(inputs, deltas):
    channels = inputs.shape[-1]
    box_side = inputs.shape[1]
    padded = jnp.pad(inputs, ((0, 0), (1, 1), (1, 1), (0, 0)))
    flat_delta = deltas.reshape(-1, channels)
    blocks = []
    for shift_y in range(3):
        for shift_x in range(3):
            window = padded[
                :, shift_y : shift_y + box_side, shift_x : shift_x + box_side, :
            ].reshape(-1, channels)
            blocks.append(
                lax.dot_general(
                    window, flat_delta, (((0,), (0,)), ((), ())), preferred_element_type=jnp.float32
                )
            )
    return jnp.stack(blocks).reshape(3, 3, channels, channels)


def pick_rows(table, values):
    flat = values.reshape(values.shape[0], -1)
    return jnp.dot(table, flat, preferred_element_type=jnp.float32).astype(jnp.bfloat16)


def pick_back(table, values):
    return lax.dot_general(
        table, values, (((0,), (0,)), ((), ())), preferred_element_type=jnp.float32
    ).astype(jnp.bfloat16)


def body(in_map, tile_w, head_w1, head_w2, box_row, box_col, box_target, head_cot):
    tile_rows, tile_cols, channels = in_map.shape
    head_count = head_cot.shape[0]
    box_side = head_cot.shape[2]
    slot_count = box_target.shape[0]
    columns = lax.axis_size("col")
    capacity = slot_count // columns
    pair_count = columns * capacity
    padded = padded_2(in_map, (("row", 0), ("col", 1)), 1)
    preact = conv_pad(padded[None], tile_w, 0)[0]
    target = box_target[:, 0]
    occupied = target >= 0
    dest_col = jnp.where(occupied, target // head_count, 0)
    head_slot = jnp.where(occupied, target % head_count, 0)
    slot_ids = jnp.arange(slot_count, dtype=jnp.int32)
    same_dest = (dest_col[:, None] == dest_col[None, :]) & occupied[None, :]
    placing = jnp.sum(same_dest & (slot_ids[None, :] < slot_ids[:, None]), axis=1)
    pair_slot = dest_col * capacity + placing
    pair_ids = jnp.arange(pair_count, dtype=jnp.int32)
    send_map = ((pair_slot[None, :] == pair_ids[:, None]) & occupied[None, :]).astype(jnp.bfloat16)
    head_ids = jnp.arange(head_count, dtype=jnp.int32)
    head_hot = ((head_slot[:, None] == head_ids[None, :]) & occupied[:, None]).astype(jnp.bfloat16)
    pair_head = (
        jnp.dot(send_map, head_hot, preferred_element_type=jnp.float32)
        .astype(jnp.bfloat16)
        .reshape(columns, capacity, head_count)
    )
    top_row = box_row[:, 0]
    left_col = box_col[:, 0]
    zero_index = jnp.zeros((), jnp.int32)
    window = box_side + 2
    windows = jax.vmap(
        lambda y, x: lax.dynamic_slice(padded, (y, x, zero_index), (window, window, channels))
    )(top_row, left_col)
    outgoing = pick_rows(send_map, windows).reshape(columns, capacity, window, window, channels)
    arrived, arrived_head = (
        lax.all_to_all(outgoing, "col", split_axis=0, concat_axis=0, tiled=True),
        lax.all_to_all(pair_head, "col", split_axis=0, concat_axis=0, tiled=True),
    )
    arrived_head = arrived_head.reshape(pair_count, head_count)
    gathered = pick_back(arrived_head, arrived.reshape(pair_count, -1)).reshape(
        head_count, window, window, channels
    )
    box_input = jax.nn.silu(conv_pad(gathered, tile_w, 0)).astype(jnp.bfloat16)
    factor = 1.0 / math.sqrt(lax.axis_size("row") * columns * head_count * box_side * box_side)
    cotangent = head_cot[:, 0]
    pre_one = conv_pad(box_input, head_w1, 1)
    hidden = jax.nn.silu(pre_one).astype(jnp.bfloat16)
    pre_two = conv_pad(hidden, head_w2, 1)
    delta_two = (cotangent.astype(jnp.float32) * silu_slope(pre_two)).astype(jnp.bfloat16)
    second_local = weight_grad(hidden, delta_two)
    delta_one = (conv_pad(delta_two, flip_weights(head_w2), 1) * silu_slope(pre_one)).astype(
        jnp.bfloat16
    )
    box_grads = conv_pad(delta_one, flip_weights(head_w1), 1).astype(jnp.bfloat16)
    sent_back = pick_rows(arrived_head, box_grads).reshape(
        columns, capacity, box_side, box_side, channels
    )
    returned = lax.all_to_all(sent_back, "col", split_axis=0, concat_axis=0, tiled=True)
    slot_grads = pick_back(send_map, returned.reshape(pair_count, -1)).reshape(
        slot_count, box_side, box_side, channels
    )
    first_local = weight_grad(box_input, delta_one)
    first_sum, second_sum = lax.psum((first_local, second_local), ("row", "col"))

    def add_box(slot, running):
        current = lax.dynamic_slice(
            running, (top_row[slot], left_col[slot], zero_index), (box_side, box_side, channels)
        )
        return lax.dynamic_update_slice(
            running,
            current + slot_grads[slot].astype(jnp.float32),
            (top_row[slot], left_col[slot], zero_index),
        )

    box_total = lax.fori_loop(
        0, slot_count, add_box, jnp.zeros((tile_rows, tile_cols, channels), jnp.float32)
    )
    delta_map = (box_total * silu_slope(preact)).astype(jnp.bfloat16)
    delta_rim = padded_2(delta_map, (("row", 0), ("col", 1)), 1)
    grad_map = conv_pad(delta_rim[None], flip_weights(tile_w), 0)[0].astype(jnp.bfloat16)
    return (grad_map, first_sum * factor, second_sum * factor)


def solution(mesh):
    in_specs = (
        P("row", "col", None),
        P(),
        P(),
        P(),
        P("row", "col"),
        P("row", "col"),
        P("row", "col"),
        P("row", "col", None, None, None),
    )
    out_specs = (P("row", "col", None), P(), P())
    return jax.shard_map(body, mesh=mesh, in_specs=in_specs, out_specs=out_specs, check_vma=False)
```

profile of v0, /device:TPU:0, one launch (start us, length us, event | category | flops | bytes accessed | tf_op | source)
XLA Modules:
  0.0 296.7 jit_solution(2329614647910186350)
XLA Ops:
  7.2 0.8 fusion.207
  8.0 1.3 collective-permute-start.1
  9.3 3.0 %collective-permute-start = (bf16[1,32,256]{2,1,0:T(8,128)(2,1)S(1)}, bf16[1,32,256]{2,1,0:T(8,128)(2,1)S(1)}, u32[]{:S(2)}, u32[]{:S(2)}) collective-permute-start(bf16[1,32,256]{2,1,0:T(8,128)(2,1)S(1)} %get-tuple-element.174), channel_id=1, source_target_pairs={{0,4},{4,8},{8,12},{12,16},{16,20},{20,24},{24,28},{1,5},{5,9},{9,... | collective-permute-start | bytes 49160 | tf_op jit(solution)/shard_map/ppermute | solution.py:18
  15.9 1.0 constant_dynamic-update-slice_fusion.1
  16.9 5.0 %collective-permute-start.2 = (bf16[18,1,256]{2,1,0:T(2,128)(2,1)S(1)}, bf16[18,1,256]{2,1,0:T(2,128)(2,1)S(1)}, u32[]{:S(2)}, u32[]{:S(2)}) collective-permute-start(bf16[18,1,256]{2,1,0:T(2,128)(2,1)S(1)} %get-tuple-element.169), channel_id=1, source_target_pairs={{0,1},{1,2},{2,3},{4,5},{5,6},{6,7},{8,9},{9,10},{10,11},{12,13},{... | collective-permute-start | bytes 27656 | tf_op jit(solution)/shard_map/ppermute | solution.py:18
  21.9 1.3 collective-permute-start.3
  23.3 4.3 %collective-permute-done.3 = bf16[18,1,256]{2,1,0:T(2,128)(2,1)S(1)} collective-permute-done((bf16[18,1,256]{2,1,0:T(2,128)(2,1)S(1)}, bf16[18,1,256]{2,1,0:T(2,128)(2,1)S(1)}, u32[]{:S(2)}, u32[]{:S(2)}) %collective-permute-start.3) | collective-permute-done | bytes 9248 | tf_op jit(solution)/shard_map/ppermute | solution.py:19
  27.8 20.0 %while.15 = (s32[]{:T(128)}, bf16[18,34,256]{2,1,0:T(8,128)(2,1)S(1)}, s32[8,3]{0,1:T(4,128)S(1)}, bf16[8,16,16,256]{3,2,1,0:T(8,128)(2,1)}, s32[]{:T(128)}) while((s32[]{:T(128)}, bf16[18,34,256]{2,1,0:T(8,128)(2,1)S(1)}, s32[8,3]{0,1:T(4,128)S(1)}, bf16[8,16,16,256]{3,2,1,0:T(8,128)(2,1)}, s32[]{:T(128)}) %tuple.64), condition=%wide.while_cond, body=%wide.while_body.sunk | while | flops 2 | bytes 263285 | solution.py:106
  28.4 1.9 bitcast_dynamic-update-slice_fusion.2
  30.9 1.9 bitcast_dynamic-update-slice_fusion.2
  33.4 1.9 bitcast_dynamic-update-slice_fusion.2
  35.9 1.9 bitcast_dynamic-update-slice_fusion.2
  38.4 1.9 bitcast_dynamic-update-slice_fusion.2
  40.9 1.9 bitcast_dynamic-update-slice_fusion.2
  43.4 1.9 bitcast_dynamic-update-slice_fusion.2
  45.9 1.9 bitcast_dynamic-update-slice_fusion.2
  47.8 1.8 copy.157
  50.0 1.2 copy.158
  51.2 4.0 %all-to-all-start.1 = ((bf16[4,2,16,16,256]{4,3,2,1,0:T(8,128)(2,1)}), bf16[4,2,16,16,256]{4,3,2,1,0:T(8,128)(2,1)S(1)}, u32[]{:S(2)}, u32[]{:S(2)}) async-start(bf16[4,2,16,16,256]{4,3,2,1,0:T(8,128)(2,1)} %bitcast.140), calls=%async_computation.1 | async-start | bytes 2097152 | tf_op jit(solution)/shard_map/all_to_all | solution.py:110
  56.4 0.9 convolution_select_fusion.3
  57.3 1.1 copy.111
  58.4 22.7 %all-to-all-done.1 = bf16[4,2,16,16,256]{4,3,2,1,0:T(8,128)(2,1)S(1)} async-done(((bf16[4,2,16,16,256]{4,3,2,1,0:T(8,128)(2,1)}), bf16[4,2,16,16,256]{4,3,2,1,0:T(8,128)(2,1)S(1)}, u32[]{:S(2)}, u32[]{:S(2)}) %all-to-all-start.1) | async-done | bytes 1048608 | tf_op jit(solution)/shard_map/all_to_all | solution.py:110
  81.0 3.4 %all-to-all-start = ((bf16[4,2,4]{2,1,0:T(2,128)(2,1)}), bf16[4,2,4]{2,1,0:T(2,128)(2,1)S(1)}, u32[]{:S(2)}, u32[]{:S(2)}) async-start(bf16[4,2,4]{2,1,0:T(2,128)(2,1)} %bitcast.9), calls=%async_computation | async-start | bytes 4096 | tf_op jit(solution)/shard_map/all_to_all | solution.py:111
  84.9 4.8 %all-to-all-done = bf16[4,2,4]{2,1,0:T(2,128)(2,1)S(1)} async-done(((bf16[4,2,4]{2,1,0:T(2,128)(2,1)}), bf16[4,2,4]{2,1,0:T(2,128)(2,1)S(1)}, u32[]{:S(2)}, u32[]{:S(2)}) %all-to-all-start) | async-done | bytes 96 | tf_op jit(solution)/shard_map/all_to_all | solution.py:111
  90.9 1.3 multiply_convert_fusion.1
  93.4 1.2 fusion.43
  94.7 1.1 select_bitcast_fusion.1
  96.4 1.3 add_multiply_fusion
  97.7 0.7 copy.100
  99.1 1.2 fusion.62
  100.3 0.8 copy-done.6
  101.6 2.9 fusion.9
  105.3 0.9 copy_bitcast_fusion.2
  106.2 2.3 copy.120
  108.4 1.2 reshape.164
  109.6 0.8 copy_bitcast_fusion
  110.4 0.9 reshape.174
  111.4 2.5 convolution_convert_fusion.4
  115.5 0.7 reshape.125
  116.3 1.8 copy.105
  118.1 3.5 %all-to-all-start.2 = ((bf16[4,2,14,14,256]{4,1,3,2,0:T(2,128)(2,1)}), bf16[4,2,14,14,256]{4,1,3,2,0:T(2,128)(2,1)S(1)}, u32[]{:S(2)}, u32[]{:S(2)}) async-start(bf16[4,2,14,14,256]{4,1,3,2,0:T(2,128)(2,1)} %copy.105), calls=%async_computation.2 | async-start | bytes 1605632 | tf_op jit(solution)/shard_map/all_to_all | solution.py:132
  121.6 1.4 fusion.28
  128.4 1.0 fusion.19
  129.4 1.0 fusion.18
  130.5 1.1 fusion.17
  131.5 1.0 fusion.16
  132.6 1.0 fusion.15
  134.0 1.3 fusion.14
  135.5 1.1 fusion.13
  136.5 1.1 fusion.12
  137.6 1.1 fusion.11
  138.6 1.8 all-to-all-done.2
  141.9 45.5 %while.14 = (s32[]{:T(128)}, f32[16,32,256]{2,0,1:T(8,128)S(1)}, s32[8]{0:T(128)S(1)}, s32[8]{0:T(128)S(1)}, bf16[8,14,14,256]{3,2,1,0:T(8,128)(2,1)S(1)}, /*index=5*/s32[]{:T(128)}, s32[]{:T(128)}, s32[]{:T(128)}, s32[]{:T(128)}) while((s32[]{:T(128)}, f32[16,32,256]{2,0,1:T(8,128)S(1)}, s32[8]{0:T(128)S(1)}, s32[8]{0:T(128)S(1)}, ...), condition=%wide.region_2.3_spmd, body=%wide.region_1.2_spmd.sunk | while | flops 100360 | bytes 1706193 | solution.py:149
  187.7 1.3 collective-permute-start.4
  188.9 1.3 collective-permute-start.5
  190.3 4.3 %collective-permute-done.5 = bf16[1,32,256]{2,0,1:T(2,128)(2,1)S(1)} collective-permute-done((bf16[1,32,256]{2,0,1:T(2,128)(2,1)S(1)}, bf16[1,32,256]{2,0,1:T(2,128)(2,1)S(1)}, u32[]{:S(2)}, u32[]{:S(2)}) %collective-permute-start.5) | collective-permute-done | bytes 16416 | tf_op jit(solution)/shard_map/ppermute | solution.py:19
  194.6 1.8 collective-permute-start.6
  196.4 1.3 collective-permute-start.7
  197.8 4.4 %collective-permute-done.7 = bf16[18,1,256]{2,0,1:T(8,128)(2,1)S(1)} collective-permute-done((bf16[18,1,256]{2,0,1:T(8,128)(2,1)S(1)}, bf16[18,1,256]{2,0,1:T(8,128)(2,1)S(1)}, u32[]{:S(2)}, u32[]{:S(2)}) %collective-permute-start.7) | collective-permute-done | bytes 9248 | tf_op jit(solution)/shard_map/ppermute | solution.py:19
  202.6 1.0 fusion.10
  203.7 0.8 copy.131
  204.5 80.3 %all-reduce.5.cloned.1.call-done = (f32[3,3,256,256]{3,2,1,0:T(8,128)}, f32[3,3,256,256]{3,2,1,0:T(8,128)}) async-done(((f32[3,3,256,256]{3,2,1,0:T(8,128)}, f32[3,3,256,256]{3,2,1,0:T(8,128)}), (f32[3,3,256,256]{3,2,1,0:T(8,128)}, f32[3,3,256,256]{3,2,1,0:T(8,128)})) %all-reduce.5.cloned.1.call-update) | async-done | bytes 4718608 | tf_op jit(solution)/shard_map/psum | solution.py:137
  284.8 3.4 %broadcast_multiply_fusion.1 = f32[3,3,256,256]{3,2,1,0:T(8,128)} fusion(f32[3,3,256,256]{3,2,1,0:T(8,128)} %get-tuple-element.153), kind=kLoop, calls=%fused_computation.29 | loop fusion | flops 589824 | bytes 4718592 | tf_op jit(solution)/shard_map/mul | solution.py:155
  288.2 1.6 broadcast_multiply_fusion
  (180 shorter events, 39.3 us)
Async XLA Ops:
  7.2 49.2 %copy-start = (bf16[3,3,256,256]{3,2,1,0:T(8,128)(2,1)S(1)}, bf16[3,3,256,256]{3,2,1,0:T(8,128)(2,1)}, u32[]{:S(2)}) copy-start(bf16[3,3,256,256]{3,2,1,0:T(8,128)(2,1)} %param.11) | copy-start | bytes 3538948
  8.0 8.8 %collective-permute-start.1 = (bf16[1,32,256]{2,1,0:T(8,128)(2,1)S(1)}, bf16[1,32,256]{2,1,0:T(8,128)(2,1)S(1)}, u32[]{:S(2)}, u32[]{:S(2)}) collective-permute-start(bf16[1,32,256]{2,1,0:T(8,128)(2,1)S(1)} %get-tuple-element.173), channel_id=1, source_target_pairs={{4,0},{8,4},{12,8},{16,12},{20,16},{24,20},{28,24},{5,1},{9,5},{13... | collective-permute-start | bytes 49160 | tf_op jit(solution)/shard_map/ppermute | solution.py:19
  9.3 6.6 %collective-permute-start = (bf16[1,32,256]{2,1,0:T(8,128)(2,1)S(1)}, bf16[1,32,256]{2,1,0:T(8,128)(2,1)S(1)}, u32[]{:S(2)}, u32[]{:S(2)}) collective-permute-start(bf16[1,32,256]{2,1,0:T(8,128)(2,1)S(1)} %get-tuple-element.174), channel_id=1, source_target_pairs={{0,4},{4,8},{8,12},{12,16},{16,20},{20,24},{24,28},{1,5},{5,9},{9,... | collective-permute-start | bytes 49160 | tf_op jit(solution)/shard_map/ppermute | solution.py:18
  16.9 6.4 %collective-permute-start.2 = (bf16[18,1,256]{2,1,0:T(2,128)(2,1)S(1)}, bf16[18,1,256]{2,1,0:T(2,128)(2,1)S(1)}, u32[]{:S(2)}, u32[]{:S(2)}) collective-permute-start(bf16[18,1,256]{2,1,0:T(2,128)(2,1)S(1)} %get-tuple-element.169), channel_id=1, source_target_pairs={{0,1},{1,2},{2,3},{4,5},{5,6},{6,7},{8,9},{9,10},{10,11},{12,13},{... | collective-permute-start | bytes 27656 | tf_op jit(solution)/shard_map/ppermute | solution.py:18
  21.9 5.7 %collective-permute-start.3 = (bf16[18,1,256]{2,1,0:T(2,128)(2,1)S(1)}, bf16[18,1,256]{2,1,0:T(2,128)(2,1)S(1)}, u32[]{:S(2)}, u32[]{:S(2)}) collective-permute-start(bf16[18,1,256]{2,1,0:T(2,128)(2,1)S(1)} %get-tuple-element.170), channel_id=1, source_target_pairs={{1,0},{2,1},{3,2},{5,4},{6,5},{7,6},{9,8},{10,9},{11,10},{13,12},{... | collective-permute-start | bytes 27656 | tf_op jit(solution)/shard_map/ppermute | solution.py:19
  50.0 5.2 %copy-start.19 = (s32[8,1]{0,1:T(1,128)S(1)}, s32[8,1]{0,1:T(1,128)}, u32[]{:S(2)}) copy-start(s32[8,1]{0,1:T(1,128)} %param.16) | copy-start | bytes 100
  51.2 5.2 %copy-start.20 = (pred[8,5]{0,1:T(8,128)(4,1)S(1)}, pred[8,5]{0,1:T(8,128)(4,1)}, u32[]{:S(2)}) copy-start(pred[8,5]{0,1:T(8,128)(4,1)} %constant.129) | copy-start | bytes 124
  51.2 29.9 %all-to-all-start.1 = ((bf16[4,2,16,16,256]{4,3,2,1,0:T(8,128)(2,1)}), bf16[4,2,16,16,256]{4,3,2,1,0:T(8,128)(2,1)S(1)}, u32[]{:S(2)}, u32[]{:S(2)}) async-start(bf16[4,2,16,16,256]{4,3,2,1,0:T(8,128)(2,1)} %bitcast.140), calls=%async_computation.1 | async-start | bytes 2097152 | tf_op jit(solution)/shard_map/all_to_all | solution.py:110
  81.0 8.7 %all-to-all-start = ((bf16[4,2,4]{2,1,0:T(2,128)(2,1)}), bf16[4,2,4]{2,1,0:T(2,128)(2,1)S(1)}, u32[]{:S(2)}, u32[]{:S(2)}) async-start(bf16[4,2,4]{2,1,0:T(2,128)(2,1)} %bitcast.9), calls=%async_computation | async-start | bytes 4096 | tf_op jit(solution)/shard_map/all_to_all | solution.py:111
  90.2 0.7 copy-start.14
  92.2 1.3 copy-start.18
  94.7 1.2 copy-start.8
  94.7 1.8 copy-start.17
  100.3 0.8 copy-start.6
  105.3 6.1 %copy-start.4 = (bf16[14,4,16,256]{3,2,1,0:T(8,128)(2,1)}, bf16[14,4,16,256]{3,2,1,0:T(8,128)(2,1)S(1)}, u32[]{:S(2)}) copy-start(bf16[14,4,16,256]{3,2,1,0:T(8,128)(2,1)S(1)} %reshape.159) | copy-start | bytes 1376260
  116.3 5.3 %copy-start.10 = (bf16[4,14,14,256]{3,2,1,0:T(8,128)(2,1)S(1)}, bf16[4,14,14,256]{3,2,1,0:T(8,128)(2,1)}, u32[]{:S(2)}) copy-start(bf16[4,14,14,256]{3,2,1,0:T(8,128)(2,1)} %copy_bitcast_fusion.2) | copy-start | bytes 1204228
  118.1 22.3 %all-to-all-start.2 = ((bf16[4,2,14,14,256]{4,1,3,2,0:T(2,128)(2,1)}), bf16[4,2,14,14,256]{4,1,3,2,0:T(2,128)(2,1)S(1)}, u32[]{:S(2)}, u32[]{:S(2)}) async-start(bf16[4,2,14,14,256]{4,1,3,2,0:T(2,128)(2,1)} %copy.105), calls=%async_computation.2 | async-start | bytes 1605632 | tf_op jit(solution)/shard_map/all_to_all | solution.py:132
  121.6 1.5 copy-start.12
  121.6 163.2 %all-reduce.5.cloned.1.call-start = ((), (), s32[]{:S(2)}) async-start(), calls=%async_computation.3 | async-start | bytes 9437184 | tf_op jit(solution)/shard_map/psum | solution.py:137
  123.4 1.0 copy-start.13
  124.5 1.0 copy-start.5
  126.2 1.0 copy-start.11
  127.2 1.0 copy-start.7
  127.2 1.2 copy-start.9
  134.0 1.5 copy-start.2
  140.6 1.3 copy-start.15
  140.6 1.3 copy-start.16
  141.9 45.5 %copy-start.3 = (f32[16,8,5,256]{3,0,2,1:T(8,128)S(1)}, f32[16,8,5,256]{3,0,2,1:T(8,128)}, u32[]{:S(2)}) copy-start(f32[16,8,5,256]{3,0,2,1:T(8,128)} %copy.111) | copy-start | bytes 1966084
  187.7 2.6 collective-permute-start.4
  188.9 5.6 %collective-permute-start.5 = (bf16[1,32,256]{2,0,1:T(2,128)(2,1)S(1)}, bf16[1,32,256]{2,0,1:T(2,128)(2,1)S(1)}, u32[]{:S(2)}, u32[]{:S(2)}) collective-permute-start(bf16[1,32,256]{2,0,1:T(2,128)(2,1)S(1)} %get-tuple-element.172), channel_id=1, source_target_pairs={{4,0},{8,4},{12,8},{16,12},{20,16},{24,20},{28,24},{5,1},{9,5},{13... | collective-permute-start | bytes 49160 | tf_op jit(solution)/shard_map/ppermute | solution.py:19
  194.6 3.2 %collective-permute-start.6 = (bf16[18,1,256]{2,0,1:T(8,128)(2,1)S(1)}, bf16[18,1,256]{2,0,1:T(8,128)(2,1)S(1)}, u32[]{:S(2)}, u32[]{:S(2)}) collective-permute-start(bf16[18,1,256]{2,0,1:T(8,128)(2,1)S(1)} %get-tuple-element.167), channel_id=1, source_target_pairs={{0,1},{1,2},{2,3},{4,5},{5,6},{6,7},{8,9},{9,10},{10,11},{12,13},{... | collective-permute-start | bytes 27656 | tf_op jit(solution)/shard_map/ppermute | solution.py:18
  196.4 5.8 %collective-permute-start.7 = (bf16[18,1,256]{2,0,1:T(8,128)(2,1)S(1)}, bf16[18,1,256]{2,0,1:T(8,128)(2,1)S(1)}, u32[]{:S(2)}, u32[]{:S(2)}) collective-permute-start(bf16[18,1,256]{2,0,1:T(8,128)(2,1)S(1)} %get-tuple-element.168), channel_id=1, source_target_pairs={{1,0},{2,1},{3,2},{5,4},{6,5},{7,6},{9,8},{10,9},{11,10},{13,12},{... | collective-permute-start | bytes 27656 | tf_op jit(solution)/shard_map/ppermute | solution.py:19
  284.8 3.4 %copy-start.1 = (f32[3,3,256,256]{3,2,1,0:T(8,128)S(1)}, f32[3,3,256,256]{3,2,1,0:T(8,128)}, u32[]{:S(2)}) copy-start(f32[3,3,256,256]{3,2,1,0:T(8,128)} %get-tuple-element.154) | copy-start | bytes 7077892
Sparse Core Ops, SparseCore 0:
  138.8 145.9 all-reduce.4
where the time goes:
time: 298 us; the launch traced here: 297 us
  waiting for transfers between devices  123 us (41%)
  local copies, waits for them, and re-layouts  60.4 us (20%)
  loops' own time  31.5 us (11%)
  starting transfers between devices  27.2 us (9%)
  matrix products  27.2 us (9%)
  between operations  14.9 us (5%)
  other arithmetic  12.8 us (4%)
    psum x1, waiting for transfers between devices, body(): lax.psum((first_local, second_local), ('row', 'col'))  80.3 us
    another operation x1, loops' own time, body(): lax.fori_loop(0, slot_count, add_box, jnp.zeros((tile_rows, tile_cols, ch...  31.5 us
    all_to_all x1, waiting for transfers between devices, body(): lax.all_to_all(outgoing, 'col', split_axis=0, concat_axis=0, tiled=True)  22.7 us
    gather x24, local copies, waits for them, and re-layouts  19.9 us
    dot_general x18, matrix products, weight_grad(): lax.dot_general(window, flat_delta, (((0,), (0,)), ((), ())), preferred_e...  14 us
    ppermute x4, waiting for transfers between devices, padded_2(): after = lax.ppermute(leading, axis, down)  13 us
    ppermute x4, starting transfers between devices, padded_2(): before = lax.ppermute(last, axis, up)  11.1 us
    conv_general_dilated x7, matrix products, conv_pad(): lax.conv_general_dilated(inputs, kernel, (1, 1), ((margin, margin), (marg...  11.1 us
  transfers between devices with their start and end apart: 12, of which 9 were waited for; matrix products, arithmetic and copies ran while one was open for 13% of the time, Pallas kernels for 0%

commit v1 on v0

v1 whole, which is shorter than its diff:
```python
import functools
import math

import jax
import jax.numpy as jnp
from jax import lax
from jax.experimental import pallas as pl
from jax.experimental.pallas import tpu as pltpu
from jax.sharding import PartitionSpec as P

LAYOUT = ("NHWC", "HWIO", "NHWC")
F32 = jnp.float32
BF16 = jnp.bfloat16
PITCH = 16


def flip_weights(kernel):
    return jnp.transpose(jnp.flip(kernel, (0, 1)), (0, 1, 3, 2))


def conv_valid(inputs, kernel):
    return lax.conv_general_dilated(
        inputs[None],
        kernel,
        (1, 1),
        ((0, 0), (0, 0)),
        dimension_numbers=LAYOUT,
        preferred_element_type=F32,
    )[0]


def slope_of(values):
    sigma = jax.nn.sigmoid(values)
    return sigma * (1.0 + values * (1.0 - sigma))


def shift_rim(shard, axis, dim):
    size, length = lax.axis_size(axis), shard.shape[dim]
    up = [(i, i + 1) for i in range(size - 1)]
    down = [(j, i) for i, j in up]
    before = lax.ppermute(lax.slice_in_dim(shard, length - 1, length, axis=dim), axis, up)
    after = lax.ppermute(lax.slice_in_dim(shard, 0, 1, axis=dim), axis, down)
    return jnp.concatenate([before, shard, after], axis=dim)


def with_rim(shard):
    return shift_rim(shift_rim(shard, "col", 1), "row", 0)


def swap(values, axis, mask, stride=1):
    size = lax.axis_size(axis)
    return lax.ppermute(values, axis, [(i, i ^ (mask * stride)) for i in range(size)])


def place_in(axis, stride, group):
    return (lax.axis_index(axis) // stride) % group


def scatter_sum(values, axis, stride):
    group = values.shape[0]
    mine = place_in(axis, stride, group)
    own = lax.dynamic_index_in_dim(values, mine, 0, keepdims=False)
    parts = [
        swap(lax.dynamic_index_in_dim(values, mine ^ m, 0, keepdims=False), axis, m, stride)
        for m in range(1, group)
    ]
    total = own.astype(F32)
    for part in parts:
        total = total + part.astype(F32)
    return total.astype(BF16)


def gather_all(piece, axis, stride, group):
    mine = place_in(axis, stride, group)
    parts = [swap(piece, axis, m, stride) for m in range(1, group)]
    whole = jnp.zeros((group,) + piece.shape, piece.dtype)
    whole = lax.dynamic_update_index_in_dim(whole, piece, mine, 0)
    for m, part in enumerate(parts, 1):
        whole = lax.dynamic_update_index_in_dim(whole, part, mine ^ m, 0)
    return whole


def levels_of(row_size, col_size):
    levels = []
    for axis, size, first in (("row", row_size, 2), ("col", col_size, 4)):
        stride, group = 1, first
        while stride < size:
            group = min(group, size // stride)
            levels.append((axis, stride, group))
            stride, group = stride * group, 4
    return levels


def sum_all(partial):
    levels = levels_of(lax.axis_size("row"), lax.axis_size("col"))
    shape = partial.shape
    groups = [group for _, _, group in levels]
    values = partial.reshape(*groups, -1, shape[-1])
    for axis, stride, _ in levels:
        values = scatter_sum(values, axis, stride)
    for axis, stride, group in reversed(levels):
        values = gather_all(values, axis, stride, group)
    return values.reshape(shape)


def vmem():
    return pl.BlockSpec(memory_space=pltpu.VMEM)


def smem():
    return pl.BlockSpec(memory_space=pltpu.SMEM)


def params():
    return pltpu.CompilerParams(vmem_limit_bytes=60 << 20)


def inside(rows, side):
    q = lax.broadcasted_iota(jnp.int32, (rows, 1), 0)
    row = lax.rem(lax.div(q, PITCH), side + 1)
    return (row < side) & (lax.rem(q, PITCH) < side)


def store_shifted(ref, start, values, channels, back):
    rows = values.shape[0]
    one = 1 if back else rows - 1
    ref[pl.ds(start, rows), 0:channels] = pltpu.roll(values, one, 0).astype(BF16)
    ref[pl.ds(start, rows), channels : 2 * channels] = values.astype(BF16)
    ref[pl.ds(start, rows), 2 * channels :] = pltpu.roll(values, rows - one, 0).astype(BF16)


def clear_ends(ref, start, rows):
    zero = jnp.zeros((PITCH, ref.shape[1]), BF16)
    ref[0:PITCH, :] = zero
    ref[start + rows : start + rows + PITCH, :] = zero


def conv_rows(ref, start, rows, weight):
    cols = jnp.concatenate(
        [ref[pl.ds(pl.multiple_of(start + a * PITCH - PITCH, PITCH), rows), :] for a in range(3)],
        axis=1,
    )
    return jnp.dot(cols, weight[...], preferred_element_type=F32)


def pick_kernel(head_ref, cot_ref, *out_refs):
    n = 0
    for out in out_refs:
        for k in range(out.shape[0]):
            out[k] = cot_ref[head_ref[n]]
            n += 1


def forward_kernel(
    side, width, anchor_ref, feature_ref, w1_ref, w2_ref,
    crop_t_ref, hidden_t_ref, slope1_ref, slope2_ref, place_ref, frame_ref, frame2_ref,
):
    cells, channels = feature_ref.shape
    boxes = anchor_ref.shape[0]
    frame = (side + 1) * PITCH
    step = 2 * frame
    total = boxes * frame
    q = lax.broadcasted_iota(jnp.int32, (frame, cells), 0)
    n = lax.broadcasted_iota(jnp.int32, (frame, cells), 1)
    row, col = lax.div(q, PITCH), lax.rem(q, PITCH)
    place_ref[...] = jnp.where((row < side) & (col < side), n - row * width - col, -1)
    clear_ends(frame_ref, PITCH, total)
    clear_ends(frame2_ref, PITCH, total)
    feature = feature_ref[...]

    def crop(p, carry):
        hot = jnp.where(place_ref[...] == anchor_ref[p], 1.0, 0.0).astype(BF16)
        values = jnp.dot(hot, feature, preferred_element_type=F32)
        start = pl.multiple_of(PITCH + p * frame, PITCH)
        store_shifted(frame_ref, start, values, channels, True)
        return carry

    lax.fori_loop(0, boxes, crop, 0)
    mask = inside(step, side)

    def one(i, carry):
        at = pl.multiple_of(i * step, PITCH)
        pre = conv_rows(frame_ref, PITCH + at, step, w1_ref)
        sigma = jax.nn.sigmoid(pre)
        slope1_ref[pl.ds(at, step), :] = sigma * (1.0 + pre * (1.0 - sigma))
        store_shifted(
            frame2_ref, pl.multiple_of(PITCH + at, PITCH), jnp.where(mask, pre * sigma, 0.0), channels, True
        )
        return carry

    lax.fori_loop(0, boxes // 2, one, 0)

    def two(i, carry):
        at = pl.multiple_of(i * step, PITCH)
        slope2_ref[pl.ds(at, step), :] = slope_of(conv_rows(frame2_ref, PITCH + at, step, w2_ref))
        return carry

    lax.fori_loop(0, boxes // 2, two, 0)
    for source, out in ((frame_ref, crop_t_ref), (frame2_ref, hidden_t_ref)):
        out[...] = source[PITCH : PITCH + total, channels : 2 * channels].T


def weight_sums(values_t_ref, frame_ref, out_ref):
    channels, total = values_t_ref.shape
    for a in range(3):
        rows = frame_ref[(2 - a) * PITCH : (2 - a) * PITCH + total, :]
        sums = jnp.dot(values_t_ref[...], rows, preferred_element_type=F32)
        for b in range(3):
            out_ref[a, b] = sums[:, b * channels : (b + 1) * channels].astype(BF16)


def second_kernel(side, valid_ref, slope_ref, hidden_t_ref, *refs):
    cots, (grad_ref, frame_ref, pad_ref) = refs[:-3], refs[-3:]
    total, channels = slope_ref.shape
    frame = (side + 1) * PITCH
    clear_ends(frame_ref, PITCH, total)
    pad_ref[...] = jnp.zeros_like(pad_ref)
    n = 0
    for cot in cots:
        for k in range(cot.shape[0]):
            pad_ref[0:side, 0:side, :] = cot[k]
            at = n * frame
            value = pad_ref[...].reshape(frame, channels).astype(F32)
            value = jnp.where(valid_ref[n] > 0, value * slope_ref[at : at + frame, :], 0.0)
            store_shifted(frame_ref, PITCH + at, value, channels, False)
            n += 1
    weight_sums(hidden_t_ref, frame_ref, grad_ref)


def first_kernel(side, slope_ref, crop_t_ref, weight_ref, frame2_ref, grad_ref, frame_ref):
    total, channels = slope_ref.shape
    step = 2 * (side + 1) * PITCH
    clear_ends(frame_ref, PITCH, total)
    mask = inside(step, side)

    def back(i, carry):
        at = pl.multiple_of(i * step, PITCH)
        value = conv_rows(frame2_ref, PITCH + at, step, weight_ref) * slope_ref[pl.ds(at, step), :]
        store_shifted(
            frame_ref, pl.multiple_of(PITCH + at, PITCH), jnp.where(mask, value, 0.0), channels, False
        )
        return carry

    lax.fori_loop(0, total // step, back, 0)
    weight_sums(crop_t_ref, frame_ref, grad_ref)


def map_kernel(side, cell_ref, slope_ref, weight_ref, frame_ref, out_ref, grads_ref):
    total = cell_ref.shape[1]
    cells, channels = out_ref.shape
    step = 2 * (side + 1) * PITCH

    def back(i, carry):
        at = pl.multiple_of(i * step, PITCH)
        grads_ref[pl.ds(at, step), :] = conv_rows(frame_ref, PITCH + at, step, weight_ref).astype(BF16)
        return carry

    lax.fori_loop(0, total // step, back, 0)
    n = lax.broadcasted_iota(jnp.int32, (cells, total), 0)
    hot = jnp.where(n == cell_ref[...], 1.0, 0.0).astype(BF16)
    sums = jnp.dot(hot, grads_ref[...], preferred_element_type=F32)
    out_ref[...] = (sums * slope_ref[...]).astype(BF16)


def ranks(match):
    ids = jnp.arange(match.shape[-1], dtype=jnp.int32)
    before = ids[None, :] < ids[:, None]
    return jnp.sum((match[..., None, :] & before).astype(jnp.int32), axis=-1)


def body(in_map, tile_w, head_w1, head_w2, box_row, box_col, box_target, head_cot):
    tile_rows, tile_cols, channels = in_map.shape
    heads, side = head_cot.shape[0], head_cot.shape[2]
    slots = box_target.shape[0]
    columns = lax.axis_size("col")
    capacity = slots // columns
    me = lax.axis_index("col")
    shape = jax.ShapeDtypeStruct
    frame = (side + 1) * PITCH
    total = slots * frame
    cells = tile_rows * tile_cols
    places = jnp.arange(capacity, dtype=jnp.int32)
    masks = jnp.arange(columns, dtype=jnp.int32)

    target = box_target[:, 0]
    tables = jnp.stack([target] + [swap(target, "col", m) for m in range(1, columns)])
    wanted = (tables >= 0) & (tables // heads == me)
    hot = wanted[:, None, :] & (ranks(wanted)[:, None, :] == places[None, :, None])
    chosen = jnp.sum(jnp.where(hot, (tables % heads)[:, None, :], 0), axis=2).reshape(-1)
    sends = pl.pallas_call(
        pick_kernel,
        out_shape=[shape((capacity,) + head_cot.shape[2:], BF16)] * columns,
        in_specs=[smem(), vmem()],
        out_specs=[vmem()] * columns,
        compiler_params=params(),
        name="pick",
    )(chosen, head_cot[:, 0])
    cots = [sends[0]] + [swap(sends[m], "col", m) for m in range(1, columns)]

    mine = (target >= 0)[None, :] & ((target // heads)[None, :] == (me ^ masks)[:, None])
    hot = mine[:, None, :] & (ranks(mine)[:, None, :] == places[None, :, None])
    corner = box_row[:, 0] * tile_cols + box_col[:, 0]
    anchor = jnp.sum(jnp.where(hot, corner[None, None, :], 0), axis=2).reshape(-1)
    valid = jnp.sum(hot.astype(jnp.int32), axis=2).reshape(-1)
    q = jnp.arange(frame, dtype=jnp.int32)
    row, col = q // PITCH, q % PITCH
    real = (row < side) & (col < side)
    cell = jnp.where(real[None, :], anchor[:, None] + (row * tile_cols + col)[None, :], -1)
    cell = cell.reshape(1, total)

    preact = conv_valid(with_rim(in_map), tile_w).reshape(cells, channels)
    feature = jax.nn.silu(preact).astype(BF16)
    map_slope = slope_of(preact)

    w1 = head_w1.reshape(-1, channels)
    w2 = head_w2.reshape(-1, channels)
    back1, back2 = (
        jnp.transpose(jnp.flip(w, (0,)), (0, 1, 3, 2)).reshape(-1, channels) for w in (head_w1, head_w2)
    )
    frames = shape((total + 2 * PITCH, 3 * channels), BF16)
    grads = shape(head_w1.shape, BF16)
    rows32 = shape((total, channels), F32)
    flops = 2 * total * 9 * channels * channels

    crop_t, hidden_t, slope1, slope2 = pl.pallas_call(
        functools.partial(forward_kernel, side, tile_cols),
        out_shape=[shape((channels, total), BF16)] * 2 + [rows32] * 2,
        in_specs=[smem()] + [vmem()] * 3,
        out_specs=[vmem()] * 4,
        scratch_shapes=[
            pltpu.VMEM((frame, cells), jnp.int32),
            pltpu.VMEM(frames.shape, BF16),
            pltpu.VMEM(frames.shape, BF16),
        ],
        compiler_params=params(),
        cost_estimate=pl.CostEstimate(flops=2 * flops, bytes_accessed=8 << 20, transcendentals=0),
        name="forward",
    )(anchor, feature, w1, w2)

    grad2, frame2 = pl.pallas_call(
        functools.partial(second_kernel, side),
        out_shape=[grads, frames],
        in_specs=[smem()] + [vmem()] * (2 + columns),
        out_specs=[vmem()] * 2,
        scratch_shapes=[pltpu.VMEM((side + 1, PITCH, channels), BF16)],
        compiler_params=params(),
        cost_estimate=pl.CostEstimate(flops=flops, bytes_accessed=8 << 20, transcendentals=0),
        name="second",
    )(valid, slope2, hidden_t, *cots)
    sum2 = sum_all(grad2)

    grad1, frame1 = pl.pallas_call(
        functools.partial(first_kernel, side),
        out_shape=[grads, frames],
        in_specs=[vmem()] * 4,
        out_specs=[vmem()] * 2,
        compiler_params=params(),
        cost_estimate=pl.CostEstimate(flops=2 * flops, bytes_accessed=8 << 20, transcendentals=0),
        name="first",
    )(slope1, crop_t, back2, frame2)
    sum1 = sum_all(grad1)

    delta_map = pl.pallas_call(
        functools.partial(map_kernel, side),
        out_shape=shape((cells, channels), BF16),
        in_specs=[vmem()] * 4,
        out_specs=vmem(),
        scratch_shapes=[pltpu.VMEM((total, channels), BF16)],
        compiler_params=params(),
        cost_estimate=pl.CostEstimate(flops=flops, bytes_accessed=8 << 20, transcendentals=0),
        name="boxes",
    )(cell, map_slope, back1, frame1)
    delta_rim = with_rim(delta_map.reshape(tile_rows, tile_cols, channels))
    grad_map = conv_valid(delta_rim, flip_weights(tile_w)).astype(BF16)

    factor = 1.0 / math.sqrt(lax.axis_size("row") * columns * heads * side * side)
    return (grad_map, sum1.astype(F32) * factor, sum2.astype(F32) * factor)


def solution(mesh):
    in_specs = (
        P("row", "col", None),
        P(),
        P(),
        P(),
        P("row", "col"),
        P("row", "col"),
        P("row", "col"),
        P("row", "col", None, None, None),
    )
    out_specs = (P("row", "col", None), P(), P())
    return jax.shard_map(body, mesh=mesh, in_specs=in_specs, out_specs=out_specs, check_vma=False)
```

time: 298 us -> 157 us (0.53)
  waiting for transfers between devices: 123 us -> 17.7 us
  local copies, waits for them, and re-layouts: 60.4 us -> 15.6 us
  starting transfers between devices: 27.2 us -> 65.9 us
  Pallas kernels: 0 us -> 37.9 us
  loops' own time: 31.5 us -> 0 us
  matrix products: 27.2 us -> 4.29 us
  between operations: 14.9 us -> 1.44 us
    psum x1 -> x0, waiting for transfers between devices: 80.3 us -> none  [body(): lax.psum((first_local, second_local), ('row', 'col'))]
    ppermute x8 -> x42, starting transfers between devices: 16.3 us -> 65.9 us  [the longest x34 52.5 us: swap(): lax.ppermute(values, axis, [(i, i ^ mask * stride) for i in range(size)])]
    pallas_call x0 -> x5, Pallas kernels: none -> 37.9 us  [the longest x1 13.2 us: body(): pl.pallas_call(functools.partial(forward_kernel, side, tile_cols), out_sh...]
    another operation x2 -> x0, loops' own time: 31.5 us -> none  [the longest x1 31.5 us: body(): lax.fori_loop(0, slot_count, add_box, jnp.zeros((tile_rows, tile_cols, ch...]
    all_to_all x3 -> x0, waiting for transfers between devices: 29.2 us -> none  [the longest x1 22.7 us: body(): lax.all_to_all(outgoing, 'col', split_axis=0, concat_axis=0, tiled=True)]
    gather x24 -> x0, local copies, waits for them, and re-layouts: 19.9 us -> none
    dot_general x23 -> x0, matrix products: 16.2 us -> none  [the longest x18 14 us: weight_grad(): lax.dot_general(window, flat_delta, (((0,), (0,)), ((), ())), preferred_e...]
    all_to_all x3 -> x0, starting transfers between devices: 10.9 us -> none  [the longest x1 3.99 us: body(): lax.all_to_all(outgoing, 'col', split_axis=0, concat_axis=0, tiled=True)]
  transfers between devices with their start and end apart: 12 -> 42, of which waited for: 9 -> 10; matrix products, arithmetic and copies ran while one was open for 13% -> 19% of each run, Pallas kernels for 0% -> 10%
where the time goes in v1:
time: 157 us; the launch traced here: 156 us
  starting transfers between devices  65.9 us (42%)
  Pallas kernels  37.9 us (24%)
  waiting for transfers between devices  17.7 us (11%)
  local copies, waits for them, and re-layouts  15.6 us (10%)
  other arithmetic  13.4 us (9%)
  matrix products  4.29 us (3%)
    ppermute x34, starting transfers between devices, swap(): lax.ppermute(values, axis, [(i, i ^ mask * stride) for i in range(size)])  52.5 us
    pallas_call x1, Pallas kernels, body(): pl.pallas_call(functools.partial(forward_kernel, side, tile_cols), out_sh...  13.2 us
    ppermute x34, waiting for transfers between devices, swap(): lax.ppermute(values, axis, [(i, i ^ mask * stride) for i in range(size)])  12.3 us
    pallas_call x1, Pallas kernels, body(): pl.pallas_call(functools.partial(first_kernel, side), out_shape=[grads, f...  9.93 us
    ppermute x4, starting transfers between devices, shift_rim(): lax.ppermute(lax.slice_in_dim(shard, length - 1, length, axis=dim), axis,...  8.05 us
    pallas_call x1, Pallas kernels, body(): pl.pallas_call(functools.partial(map_kernel, side), out_shape=shape((cell...  6.85 us
    pallas_call x1, Pallas kernels, body(): pl.pallas_call(functools.partial(second_kernel, side), out_shape=[grads,...  5.9 us
    ppermute x4, waiting for transfers between devices, shift_rim(): after = lax.ppermute(lax.slice_in_dim(shard, 0, 1, axis=dim), axis, down)  5.45 us
  transfers between devices with their start and end apart: 42, of which 10 were waited for; matrix products, arithmetic and copies ran while one was open for 19% of the time, Pallas kernels for 10%

profile of v1, /device:TPU:0, one launch (start us, length us, event | category | flops | bytes accessed | tf_op | source)
XLA Modules:
  0.0 156.3 jit_solution(2721307269853617845)
XLA Ops:
  0.6 3.1 %collective-permute-start.4 = (s32[8]{0:T(128)}, s32[8]{0:T(128)}, u32[]{:S(2)}, u32[]{:S(2)}) collective-permute-start(s32[8]{0:T(128)} %bitcast.161), channel_id=1, source_target_pairs={{0,1},{1,0},{2,3},{3,2},{4,5},{5,4},{6,7},{7,6},{8,9},{9,8},{10,11... | collective-permute-start | bytes 104 | tf_op jit(solution)/shard_map/ppermute | solution.py:52
  3.8 2.6 %collective-permute-start.5 = (s32[8]{0:T(128)}, s32[8]{0:T(128)}, u32[]{:S(2)}, u32[]{:S(2)}) collective-permute-start(s32[8]{0:T(128)} %bitcast.162), channel_id=1, source_target_pairs={{0,2},{1,3},{2,0},{3,1},{4,6},{5,7},{6,4},{7,5},{8,10},{9,11},{10,... | collective-permute-start | bytes 104 | tf_op jit(solution)/shard_map/ppermute | solution.py:52
  6.4 1.5 fusion.44
  7.9 2.8 %collective-permute-start = (bf16[16,1,256]{2,1,0:T(2,128)(2,1)}, bf16[16,1,256]{2,1,0:T(2,128)(2,1)S(1)}, u32[]{:S(2)}, u32[]{:S(2)}) collective-permute-start(bf16[16,1,256]{2,1,0:T(2,128)(2,1)} %get-tuple-element.55), channel_id=1, source_target_pairs={{0,1},{1,2},{2,3},{4,5},{5,6},{6,7},{8,9},{9,10},{10,11},{12,13},{... | collective-permute-start | bytes 24584 | tf_op jit(solution)/shard_map/ppermute | solution.py:41
  10.7 1.3 collective-permute-start.1
  12.0 1.2 and_select_fusion
  13.1 1.3 broadcast_compare_fusion.1
  16.7 1.8 %copy.46 = bf16[4,1,14,14,256]{4,3,2,0,1:T(8,128)(2,1)} copy(bf16[4,1,14,14,256]{4,0,3,2,1:T(4,128)(2,1)} %param.15) | data formatting | bytes 802816 | tf_op args[7]
  18.5 1.3 reverse_bitcast_fusion
  19.8 1.6 copy.28
  21.6 1.5 copy.27
  23.3 0.7 compare_and_fusion
  26.1 2.0 %pick.1 = (bf16[2,14,14,256]{3,2,1,0:T(8,128)(2,1)}, bf16[2,14,14,256]{3,2,1,0:T(8,128)(2,1)}, bf16[2,14,14,256]{3,2,1,0:T(8,128)(2,1)}, bf16[2,14,14,256]{3,2,1,0:T(8,128)(2,1)}) custom-call(s32[8]{0:T(128)} %reshape.461.head_ref, bf16[4,14,14,256]{3,2,1,0:T(8,128)(2,1)} %bitcast.149), custom_call_target="tpu_custom_call" | custom-call | tf_op jit(solution)/shard_map/pick/pallas_call | solution.py:290
  28.1 2.6 %collective-permute-start.7 = (bf16[2,14,14,256]{3,2,1,0:T(8,128)(2,1)}, bf16[2,14,14,256]{3,2,1,0:T(8,128)(2,1)S(1)}, u32[]{:S(2)}, u32[]{:S(2)}) collective-permute-start(bf16[2,14,14,256]{3,2,1,0:T(8,128)(2,1)} %get-tuple-element.20), channel_id=1, source_target_pairs={{0,1},{1,0},{2,3},{3,2},{4,5},{5,4},{6,7},{7,6},{8,9},{9,8},{10,11... | collective-permute-start | bytes 602120 | tf_op jit(solution)/shard_map/ppermute | solution.py:52
  30.7 4.1 %collective-permute-start.8 = (bf16[2,14,14,256]{3,2,1,0:T(8,128)(2,1)}, bf16[2,14,14,256]{3,2,1,0:T(8,128)(2,1)S(1)}, u32[]{:S(2)}, u32[]{:S(2)}) collective-permute-start(bf16[2,14,14,256]{3,2,1,0:T(8,128)(2,1)} %get-tuple-element.21), channel_id=1, source_target_pairs={{0,2},{1,3},{2,0},{3,1},{4,6},{5,7},{6,4},{7,5},{8,10},{9,11},{10,... | collective-permute-start | bytes 602120 | tf_op jit(solution)/shard_map/ppermute | solution.py:52
  35.5 1.3 collective-permute-start.2
  36.8 1.5 collective-permute-start.3
  39.8 1.8 %collective-permute-done.3 = bf16[1,34,256]{2,1,0:T(8,128)(2,1)S(1)} collective-permute-done((bf16[1,34,256]{2,1,0:T(8,128)(2,1)S(1)}, bf16[1,34,256]{2,1,0:T(8,128)(2,1)S(1)}, u32[]{:S(2)}, u32[]{:S(2)}) %collective-permute-start.3) | collective-permute-done | bytes 17440 | tf_op jit(solution)/shard_map/ppermute | solution.py:42
  41.6 0.9 maximum_bitcast_fusion.1
  42.5 3.3 %fusion.4 = f32[1,16,32,256]{3,0,2,1:T(1,128)S(1)} fusion(bf16[3,3,256,256]{3,2,1,0:T(8,128)(2,1)S(1)} %copy-done, bf16[1,18,34,256]{3,2,1,0:T(8,128)(2,1)S(1)} %maximum_bitcast_fusion.1), kind=kOutput, calls=%fused_computation.12 | convolution fusion | flops 603979776 | bytes 2017280 | tf_op jit(solution)/shard_map/conv_general_dilated | solution.py:22
  45.9 1.1 fusion.11
  47.0 13.2 %forward.1 = (bf16[256,1920]{1,0:T(8,128)(2,1)}, bf16[256,1920]{1,0:T(8,128)(2,1)}, f32[1920,256]{1,0:T(8,128)}, f32[1920,256]{1,0:T(8,128)}) custom-call(s32[8]{0:T(128)} %copy-done.5, bf16[512,256]{1,0:T(8,128)(2,1)} %get-tuple-element.47.feature_ref, bf16[2304,256]{1,0:T(8,128)(2,1)} %bitcast.150, bf16[2304,256]{1,0:T(8,128)(2,1)} %bitcast.151), custom_call_target="tpu_custom_call" | custom-call | flops 4529848320 | bytes 8388608 | tf_op jit(solution)/shard_map/forward/pallas_call | solution.py:325
  61.0 5.9 %second.1 = (bf16[3,3,256,256]{3,2,1,0:T(8,128)(2,1)}, bf16[1952,768]{1,0:T(8,128)(2,1)}) custom-call(s32[8]{0:T(128)} %reshape.460.valid_ref, f32[1920,256]{1,0:T(8,128)} %get-tuple-element.17.slope_ref, bf16[256,1920]{1,0:T(8,128)(2,1)} %get-tuple-element.18.hidden_t_ref, bf16[2,14,14,256]{3,2,1,0:T(8,128)(2,1)} %get-tuple-element.19.refs_0_, ...), custom_call_target="tpu_custom_call" | custom-call | flops 2264924160 | bytes 8388608 | tf_op jit(solution)/shard_map/second/pallas_call | solution.py:340
  66.9 9.9 %first.1 = (bf16[3,3,256,256]{3,2,1,0:T(8,128)(2,1)}, bf16[1952,768]{1,0:T(8,128)(2,1)}) custom-call(f32[1920,256]{1,0:T(8,128)} %get-tuple-element.15.slope_ref, bf16[256,1920]{1,0:T(8,128)(2,1)} %get-tuple-element.16.crop_t_ref, bf16[2304,256]{1,0:T(8,128)(2,1)} %bitcast.153, bf16[1952,768]{1,0:T(8,128)(2,1)} %get-tuple-element.23.frame2_ref), custom_call_target="tpu_custom_call" | custom-call | flops 4529848320 | bytes 8388608 | tf_op jit(solution)/shard_map/first/pallas_call | solution.py:352
  76.9 6.9 %boxes.1 = bf16[512,256]{1,0:T(8,128)(2,1)} custom-call(s32[1,1920]{1,0:T(1,128)} %select_n.198.cell_ref, f32[512,256]{1,0:T(8,128)} %get-tuple-element.48.slope_ref, bf16[2304,256]{1,0:T(8,128)(2,1)} %bitcast.152, bf16[1952,768]{1,0:T(8,128)(2,1)} %get-tuple-element.24.frame_ref), custom_call_target="tpu_custom_call" | custom-call | flops 2264924160 | bytes 8388608 | tf_op jit(solution)/shard_map/boxes/pallas_call | solution.py:363
  83.7 1.0 fusion.43
  84.7 2.7 %collective-permute-start.10 = (bf16[16,1,256]{2,0,1:T(8,128)(2,1)S(1)}, bf16[16,1,256]{2,0,1:T(8,128)(2,1)S(1)}, u32[]{:S(2)}, u32[]{:S(2)}) collective-permute-start(bf16[16,1,256]{2,0,1:T(8,128)(2,1)S(1)} %copy.44), channel_id=1, source_target_pairs={{0,1},{1,2},{2,3},{4,5},{5,6},{6,7},{8,9},{9,10},{10,11},{12,13},{... | collective-permute-start | bytes 24584 | tf_op jit(solution)/shard_map/ppermute | solution.py:41
  87.5 2.6 %collective-permute-start.28 = (bf16[4,4,72,256]{3,2,1,0:T(8,128)(2,1)S(1)}, bf16[4,4,72,256]{3,2,1,0:T(8,128)(2,1)S(1)}, u32[]{:S(2)}, u32[]{:S(2)}) collective-permute-start(bf16[4,4,72,256]{3,2,1,0:T(8,128)(2,1)S(1)} %dynamic-slice_bitcast_fusion), channel_id=1, source_target_pairs={{0,4},{4,0},{8,12},{12,8},{16,20},{20,16},{24,28},{28,24},{1,5},{5... | collective-permute-start | bytes 1769480 | tf_op jit(solution)/shard_map/ppermute | solution.py:52
  90.1 1.3 collective-permute-start.11
  91.4 1.1 constant_dynamic-update-slice_fusion.1
  92.5 3.1 %collective-permute-done.11 = bf16[16,1,256]{2,0,1:T(8,128)(2,1)S(1)} collective-permute-done((bf16[16,1,256]{2,0,1:T(8,128)(2,1)S(1)}, bf16[16,1,256]{2,0,1:T(8,128)(2,1)S(1)}, u32[]{:S(2)}, u32[]{:S(2)}) %collective-permute-start.11) | collective-permute-done | bytes 8224 | tf_op jit(solution)/shard_map/ppermute | solution.py:42
  95.7 1.3 collective-permute-start.12
  97.0 1.3 collective-permute-start.13
  98.3 3.8 %collective-permute-start.14 = (bf16[4,4,72,256]{3,2,1,0:T(8,128)(2,1)S(1)}, bf16[4,4,72,256]{3,2,1,0:T(8,128)(2,1)S(1)}, u32[]{:S(2)}, u32[]{:S(2)}) collective-permute-start(bf16[4,4,72,256]{3,2,1,0:T(8,128)(2,1)S(1)} %dynamic-slice_bitcast_fusion.1), channel_id=1, source_target_pairs={{0,4},{4,0},{8,12},{12,8},{16,20},{20,16},{24,28},{28,24},{1,5},{5... | collective-permute-start | bytes 1769480 | tf_op jit(solution)/shard_map/ppermute | solution.py:52
  103.7 1.0 fusion
  104.7 0.8 copy.38
  105.7 2.6 %collective-permute-start.29 = (bf16[4,72,256]{2,1,0:T(8,128)(2,1)S(1)}, bf16[4,72,256]{2,1,0:T(8,128)(2,1)S(1)}, u32[]{:S(2)}, u32[]{:S(2)}) collective-permute-start(bf16[4,72,256]{2,1,0:T(8,128)(2,1)S(1)} %get-tuple-element.41), channel_id=1, source_target_pairs={{0,8},{4,12},{8,0},{12,4},{16,24},{20,28},{24,16},{28,20},{1,9},{5... | collective-permute-start | bytes 442376 | tf_op jit(solution)/shard_map/ppermute | solution.py:52
  108.4 1.4 collective-permute-start.31
  110.1 2.0 %collective-permute-start.15 = (bf16[4,72,256]{2,1,0:T(8,128)(2,1)S(1)}, bf16[4,72,256]{2,1,0:T(8,128)(2,1)S(1)}, u32[]{:S(2)}, u32[]{:S(2)}) collective-permute-start(bf16[4,72,256]{2,1,0:T(8,128)(2,1)S(1)} %get-tuple-element.44), channel_id=1, source_target_pairs={{0,8},{4,12},{8,0},{12,4},{16,24},{20,28},{24,16},{28,20},{1,9},{5... | collective-permute-start | bytes 442376 | tf_op jit(solution)/shard_map/ppermute | solution.py:52
  112.2 1.4 collective-permute-start.17
  113.7 4.2 %collective-permute-done.30 = bf16[4,72,256]{2,1,0:T(8,128)(2,1)S(1)} collective-permute-done((bf16[4,72,256]{2,1,0:T(8,128)(2,1)S(1)}, bf16[4,72,256]{2,1,0:T(8,128)(2,1)S(1)}, u32[]{:S(2)}, u32[]{:S(2)}) %collective-permute-start.30) | collective-permute-done | bytes 147488 | tf_op jit(solution)/shard_map/ppermute | solution.py:52
  118.0 2.4 %collective-permute-start.32 = (bf16[72,256]{1,0:T(8,128)(2,1)S(1)}, bf16[72,256]{1,0:T(8,128)(2,1)S(1)}, u32[]{:S(2)}, u32[]{:S(2)}) collective-permute-start(bf16[72,256]{1,0:T(8,128)(2,1)S(1)} %get-tuple-element.57), channel_id=1, source_target_pairs={{0,1},{1,0},{2,3},{3,2},{4,5},{5,4},{6,7},{7,6},{8,9},{9,8},{10,11... | collective-permute-start | bytes 110600 | tf_op jit(solution)/shard_map/ppermute | solution.py:52
  120.4 1.5 collective-permute-start.33
  122.0 1.4 collective-permute-start.34
  123.3 0.8 collective-permute-done.16
  124.3 2.4 %collective-permute-start.18 = (bf16[72,256]{1,0:T(8,128)(2,1)S(1)}, bf16[72,256]{1,0:T(8,128)(2,1)S(1)}, u32[]{:S(2)}, u32[]{:S(2)}) collective-permute-start(bf16[72,256]{1,0:T(8,128)(2,1)S(1)} %get-tuple-element.60), channel_id=1, source_target_pairs={{0,1},{1,0},{2,3},{3,2},{4,5},{5,4},{6,7},{7,6},{8,9},{9,8},{10,11... | collective-permute-start | bytes 110600 | tf_op jit(solution)/shard_map/ppermute | solution.py:52
  126.7 1.5 collective-permute-start.19
  128.3 1.4 collective-permute-start.20
  130.4 2.4 %collective-permute-start.36 = (bf16[72,256]{1,0:T(8,128)(2,1)S(1)}, bf16[72,256]{1,0:T(8,128)(2,1)S(1)}, u32[]{:S(2)}, u32[]{:S(2)}) collective-permute-start(bf16[72,256]{1,0:T(8,128)(2,1)S(1)} %get-tuple-element.38), channel_id=1, source_target_pairs={{0,2},{1,3},{2,0},{3,1},{4,6},{5,7},{6,4},{7,5},{8,10},{9,11},{10,... | collective-permute-start | bytes 110600 | tf_op jit(solution)/shard_map/ppermute | solution.py:52
  132.8 1.4 collective-permute-start.37
  134.2 1.2 collective-permute-start.21
  135.5 1.8 %collective-permute-start.22 = (bf16[72,256]{1,0:T(8,128)(2,1)S(1)}, bf16[72,256]{1,0:T(8,128)(2,1)S(1)}, u32[]{:S(2)}, u32[]{:S(2)}) collective-permute-start(bf16[72,256]{1,0:T(8,128)(2,1)S(1)} %get-tuple-element.40), channel_id=1, source_target_pairs={{0,2},{1,3},{2,0},{3,1},{4,6},{5,7},{6,4},{7,5},{8,10},{9,11},{10,... | collective-permute-start | bytes 110600 | tf_op jit(solution)/shard_map/ppermute | solution.py:52
  137.3 1.4 collective-permute-start.23
  138.8 1.3 collective-permute-start.39
  140.1 2.2 %collective-permute-start.40 = (bf16[4,72,256]{2,1,0:T(8,128)(2,1)S(1)}, bf16[4,72,256]{2,1,0:T(8,128)(2,1)S(1)}, u32[]{:S(2)}, u32[]{:S(2)}) collective-permute-start(bf16[4,72,256]{2,1,0:T(8,128)(2,1)S(1)} %bitcast_dynamic-update-slice_fusion.12), channel_id=1, source_target_pairs={{0,24},{4,28},{8,16},{12,20},{16,8},{20,12},{24,0},{28,4},{1,25},{... | collective-permute-start | bytes 442376 | tf_op jit(solution)/shard_map/ppermute | solution.py:52
  142.3 0.7 collective-permute-done.23
  143.1 1.2 collective-permute-start.25
  144.4 0.9 collective-permute-done.38
  145.3 1.5 collective-permute-start.26
  146.8 1.6 %collective-permute-done.40 = bf16[4,72,256]{2,1,0:T(8,128)(2,1)S(1)} collective-permute-done((bf16[4,72,256]{2,1,0:T(8,128)(2,1)S(1)}, bf16[4,72,256]{2,1,0:T(8,128)(2,1)S(1)}, u32[]{:S(2)}, u32[]{:S(2)}) %collective-permute-start.40) | collective-permute-done | bytes 147488 | tf_op jit(solution)/shard_map/ppermute | solution.py:52
  148.5 1.9 %collective-permute-done.24 = bf16[4,72,256]{2,1,0:T(8,128)(2,1)S(1)} collective-permute-done((bf16[4,72,256]{2,1,0:T(8,128)(2,1)S(1)}, bf16[4,72,256]{2,1,0:T(8,128)(2,1)S(1)}, u32[]{:S(2)}, u32[]{:S(2)}) %collective-permute-start.24) | collective-permute-done | bytes 147488 | tf_op jit(solution)/shard_map/ppermute | solution.py:52
  150.5 2.0 %collective-permute-done.25 = bf16[4,72,256]{2,1,0:T(8,128)(2,1)S(1)} collective-permute-done((bf16[4,72,256]{2,1,0:T(8,128)(2,1)S(1)}, bf16[4,72,256]{2,1,0:T(8,128)(2,1)S(1)}, u32[]{:S(2)}, u32[]{:S(2)}) %collective-permute-start.25) | collective-permute-done | bytes 147488 | tf_op jit(solution)/shard_map/ppermute | solution.py:52
  153.0 1.6 %convert_multiply_fusion = f32[2,4,4,72,256]{4,3,2,1,0:T(8,128)} fusion(bf16[2,4,4,72,256]{4,3,2,1,0:T(8,128)(2,1)S(1)} %bitcast_dynamic-update-slice_fusion), kind=kLoop, calls=%fused_computation | loop fusion | flops 1179648 | bytes 3538944 | tf_op jit(solution)/shard_map/mul | solution.py:377
  154.7 1.6 %convert_multiply_fusion.1 = f32[2,4,4,72,256]{4,3,2,1,0:T(8,128)} fusion(bf16[2,4,4,72,256]{4,3,2,1,0:T(8,128)(2,1)S(1)} %bitcast_dynamic-update-slice_fusion.2), kind=kLoop, calls=%fused_computation.1 | loop fusion | flops 1179648 | bytes 3538944 | tf_op jit(solution)/shard_map/mul | solution.py:377
  (147 shorter events, 11.7 us)
Async XLA Ops:
  0.6 41.9 %copy-start = (bf16[3,3,256,256]{3,2,1,0:T(8,128)(2,1)S(1)}, bf16[3,3,256,256]{3,2,1,0:T(8,128)(2,1)}, u32[]{:S(2)}) copy-start(bf16[3,3,256,256]{3,2,1,0:T(8,128)(2,1)} %param.9) | copy-start | bytes 3538948
  0.6 22.7 %collective-permute-start.4 = (s32[8]{0:T(128)}, s32[8]{0:T(128)}, u32[]{:S(2)}, u32[]{:S(2)}) collective-permute-start(s32[8]{0:T(128)} %bitcast.161), channel_id=1, source_target_pairs={{0,1},{1,0},{2,3},{3,2},{4,5},{5,4},{6,7},{7,6},{8,9},{9,8},{10,11... | collective-permute-start | bytes 104 | tf_op jit(solution)/shard_map/ppermute | solution.py:52
  3.8 19.5 %collective-permute-start.5 = (s32[8]{0:T(128)}, s32[8]{0:T(128)}, u32[]{:S(2)}, u32[]{:S(2)}) collective-permute-start(s32[8]{0:T(128)} %bitcast.162), channel_id=1, source_target_pairs={{0,2},{1,3},{2,0},{3,1},{4,6},{5,7},{6,4},{7,5},{8,10},{9,11},{10,... | collective-permute-start | bytes 104 | tf_op jit(solution)/shard_map/ppermute | solution.py:52
  6.4 17.0 %collective-permute-start.6 = (s32[8]{0:T(128)}, s32[8]{0:T(128)}, u32[]{:S(2)}, u32[]{:S(2)}) collective-permute-start(s32[8]{0:T(128)} %bitcast.163), channel_id=1, source_target_pairs={{0,3},{1,2},{2,1},{3,0},{4,7},{5,6},{6,5},{7,4},{8,11},{9,10},{10,... | collective-permute-start | bytes 104 | tf_op jit(solution)/shard_map/ppermute | solution.py:52
  7.9 26.9 %collective-permute-start = (bf16[16,1,256]{2,1,0:T(2,128)(2,1)}, bf16[16,1,256]{2,1,0:T(2,128)(2,1)S(1)}, u32[]{:S(2)}, u32[]{:S(2)}) collective-permute-start(bf16[16,1,256]{2,1,0:T(2,128)(2,1)} %get-tuple-element.55), channel_id=1, source_target_pairs={{0,1},{1,2},{2,3},{4,5},{5,6},{6,7},{8,9},{9,10},{10,11},{12,13},{... | collective-permute-start | bytes 24584 | tf_op jit(solution)/shard_map/ppermute | solution.py:41
  10.7 24.2 %collective-permute-start.1 = (bf16[16,1,256]{2,1,0:T(2,128)(2,1)}, bf16[16,1,256]{2,1,0:T(2,128)(2,1)}, u32[]{:S(2)}, u32[]{:S(2)}) collective-permute-start(bf16[16,1,256]{2,1,0:T(2,128)(2,1)} %get-tuple-element.56), channel_id=1, source_target_pairs={{1,0},{2,1},{3,2},{5,4},{6,5},{7,6},{9,8},{10,9},{11,10},{13,12},{... | collective-permute-start | bytes 24584 | tf_op jit(solution)/shard_map/ppermute | solution.py:42
  19.8 1.6 %copy-start.2 = (bf16[3,3,256,256]{3,2,1,0:T(8,128)(2,1)S(1)}, bf16[3,3,256,256]{3,2,1,0:T(8,128)(2,1)}, u32[]{:S(2)}) copy-start(bf16[3,3,256,256]{3,2,1,0:T(8,128)(2,1)} %param.10) | copy-start | bytes 3538948
  21.5 1.6 %copy-start.16 = (s32[8,1]{0,1:T(1,128)S(1)}, s32[8,1]{0,1:T(1,128)}, u32[]{:S(2)}) copy-start(s32[8,1]{0,1:T(1,128)} %param.13) | copy-start | bytes 100
  21.5 1.6 %copy-start.17 = (s32[8,1]{0,1:T(1,128)S(1)}, s32[8,1]{0,1:T(1,128)}, u32[]{:S(2)}) copy-start(s32[8,1]{0,1:T(1,128)} %param.12) | copy-start | bytes 100
  21.5 1.7 %copy-start.10 = (s32[8]{0:T(128)S(1)}, s32[8]{0:T(128)}, u32[]{:S(2)}) copy-start(s32[8]{0:T(128)} %and_select_fusion) | copy-start | bytes 100
  21.5 1.7 %copy-start.11 = (pred[8]{0:T(512)(128)(4,1)S(1)}, pred[8]{0:T(512)(128)(4,1)}, u32[]{:S(2)}) copy-start(pred[8]{0:T(512)(128)(4,1)} %broadcast_compare_fusion.1) | copy-start | bytes 28
  21.5 1.7 %copy-start.12 = (s32[4]{0:T(128)S(1)}, s32[4]{0:T(128)}, u32[]{:S(2)}) copy-start(s32[4]{0:T(128)} %iota_xor_fusion) | copy-start | bytes 52
  21.5 1.8 %copy-start.6 = (s32[8,1]{0,1:T(1,128)S(1)}, s32[8,1]{0,1:T(1,128)}, u32[]{:S(2)}) copy-start(s32[8,1]{0,1:T(1,128)} %param.14) | copy-start | bytes 100
  21.6 3.2 %copy-start.8 = (pred[8,8]{1,0:T(8,128)(4,1)S(1)}, pred[8,8]{1,0:T(8,128)(4,1)}, u32[]{:S(2)}) copy-start(pred[8,8]{1,0:T(8,128)(4,1)} %iota_compare_fusion.3) | copy-start | bytes 196
  21.6 13.3 %copy-start.1 = (bf16[16,32,256]{2,1,0:T(8,128)(2,1)S(1)}, bf16[16,32,256]{2,1,0:T(8,128)(2,1)}, u32[]{:S(2)}) copy-start(bf16[16,32,256]{2,1,0:T(8,128)(2,1)} %param.8) | copy-start | bytes 786436
  21.6 16.7 %copy-start.7 = (s32[240]{0:T(256)S(1)}, s32[240]{0:T(256)}, u32[]{:S(2)}) copy-start(s32[240]{0:T(256)} %multiply_add_fusion) | copy-start | bytes 2884
  21.6 16.7 %copy-start.9 = (pred[240]{0:T(512)(128)(4,1)S(1)}, pred[240]{0:T(512)(128)(4,1)}, u32[]{:S(2)}) copy-start(pred[240]{0:T(512)(128)(4,1)} %compare_and_fusion.2) | copy-start | bytes 724
  25.4 20.5 %copy-start.5 = (s32[8]{0:T(128)}, s32[8]{0:T(128)S(1)}, u32[]{:S(2)}) copy-start(s32[8]{0:T(128)S(1)} %add.224.anchor_ref) | copy-start | bytes 100
  28.1 32.1 %collective-permute-start.7 = (bf16[2,14,14,256]{3,2,1,0:T(8,128)(2,1)}, bf16[2,14,14,256]{3,2,1,0:T(8,128)(2,1)S(1)}, u32[]{:S(2)}, u32[]{:S(2)}) collective-permute-start(bf16[2,14,14,256]{3,2,1,0:T(8,128)(2,1)} %get-tuple-element.20), channel_id=1, source_target_pairs={{0,1},{1,0},{2,3},{3,2},{4,5},{5,4},{6,7},{7,6},{8,9},{9,8},{10,11... | collective-permute-start | bytes 602120 | tf_op jit(solution)/shard_map/ppermute | solution.py:52
  30.7 29.4 %collective-permute-start.8 = (bf16[2,14,14,256]{3,2,1,0:T(8,128)(2,1)}, bf16[2,14,14,256]{3,2,1,0:T(8,128)(2,1)S(1)}, u32[]{:S(2)}, u32[]{:S(2)}) collective-permute-start(bf16[2,14,14,256]{3,2,1,0:T(8,128)(2,1)} %get-tuple-element.21), channel_id=1, source_target_pairs={{0,2},{1,3},{2,0},{3,1},{4,6},{5,7},{6,4},{7,5},{8,10},{9,11},{10,... | collective-permute-start | bytes 602120 | tf_op jit(solution)/shard_map/ppermute | solution.py:52
  34.8 25.4 %collective-permute-start.9 = (bf16[2,14,14,256]{3,2,1,0:T(8,128)(2,1)}, bf16[2,14,14,256]{3,2,1,0:T(8,128)(2,1)S(1)}, u32[]{:S(2)}, u32[]{:S(2)}) collective-permute-start(bf16[2,14,14,256]{3,2,1,0:T(8,128)(2,1)} %get-tuple-element.22), channel_id=1, source_target_pairs={{0,3},{1,2},{2,1},{3,0},{4,7},{5,6},{6,5},{7,4},{8,11},{9,10},{10,... | collective-permute-start | bytes 602120 | tf_op jit(solution)/shard_map/ppermute | solution.py:52
  35.5 4.3 %collective-permute-start.2 = (bf16[1,34,256]{2,1,0:T(8,128)(2,1)S(1)}, bf16[1,34,256]{2,1,0:T(8,128)(2,1)S(1)}, u32[]{:S(2)}, u32[]{:S(2)}) collective-permute-start(bf16[1,34,256]{2,1,0:T(8,128)(2,1)S(1)} %get-tuple-element.49), channel_id=1, source_target_pairs={{0,4},{4,8},{8,12},{12,16},{16,20},{20,24},{24,28},{1,5},{5,9},{9,... | collective-permute-start | bytes 52232 | tf_op jit(solution)/shard_map/ppermute | solution.py:41
  36.8 4.8 %collective-permute-start.3 = (bf16[1,34,256]{2,1,0:T(8,128)(2,1)S(1)}, bf16[1,34,256]{2,1,0:T(8,128)(2,1)S(1)}, u32[]{:S(2)}, u32[]{:S(2)}) collective-permute-start(bf16[1,34,256]{2,1,0:T(8,128)(2,1)S(1)} %get-tuple-element.50), channel_id=1, source_target_pairs={{4,0},{8,4},{12,8},{16,12},{20,16},{24,20},{28,24},{5,1},{9,5},{13... | collective-permute-start | bytes 52232 | tf_op jit(solution)/shard_map/ppermute | solution.py:42
  60.2 0.7 copy-start.13
  60.2 0.8 copy-start.14
  60.2 0.8 copy-start.15
  76.9 10.6 %copy-start.4 = (bf16[3,3,256,256]{3,2,1,0:T(8,128)(2,1)S(1)}, bf16[3,3,256,256]{3,2,1,0:T(8,128)(2,1)}, u32[]{:S(2)}) copy-start(bf16[3,3,256,256]{3,2,1,0:T(8,128)(2,1)} %get-tuple-element.26) | copy-start | bytes 3538948
  83.7 14.6 %copy-start.3 = (bf16[3,3,256,256]{3,2,1,0:T(8,128)(2,1)S(1)}, bf16[3,3,256,256]{3,2,1,0:T(8,128)(2,1)}, u32[]{:S(2)}) copy-start(bf16[3,3,256,256]{3,2,1,0:T(8,128)(2,1)} %get-tuple-element.25) | copy-start | bytes 3538948
  84.7 6.6 %collective-permute-start.10 = (bf16[16,1,256]{2,0,1:T(8,128)(2,1)S(1)}, bf16[16,1,256]{2,0,1:T(8,128)(2,1)S(1)}, u32[]{:S(2)}, u32[]{:S(2)}) collective-permute-start(bf16[16,1,256]{2,0,1:T(8,128)(2,1)S(1)} %copy.44), channel_id=1, source_target_pairs={{0,1},{1,2},{2,3},{4,5},{5,6},{6,7},{8,9},{9,10},{10,11},{12,13},{... | collective-permute-start | bytes 24584 | tf_op jit(solution)/shard_map/ppermute | solution.py:41
  87.5 18.0 %collective-permute-start.28 = (bf16[4,4,72,256]{3,2,1,0:T(8,128)(2,1)S(1)}, bf16[4,4,72,256]{3,2,1,0:T(8,128)(2,1)S(1)}, u32[]{:S(2)}, u32[]{:S(2)}) collective-permute-start(bf16[4,4,72,256]{3,2,1,0:T(8,128)(2,1)S(1)} %dynamic-slice_bitcast_fusion), channel_id=1, source_target_pairs={{0,4},{4,0},{8,12},{12,8},{16,20},{20,16},{24,28},{28,24},{1,5},{5... | collective-permute-start | bytes 1769480 | tf_op jit(solution)/shard_map/ppermute | solution.py:52
  90.1 5.5 %collective-permute-start.11 = (bf16[16,1,256]{2,0,1:T(8,128)(2,1)S(1)}, bf16[16,1,256]{2,0,1:T(8,128)(2,1)S(1)}, u32[]{:S(2)}, u32[]{:S(2)}) collective-permute-start(bf16[16,1,256]{2,0,1:T(8,128)(2,1)S(1)} %copy.45), channel_id=1, source_target_pairs={{1,0},{2,1},{3,2},{5,4},{6,5},{7,6},{9,8},{10,9},{11,10},{13,12},{... | collective-permute-start | bytes 24584 | tf_op jit(solution)/shard_map/ppermute | solution.py:42
  95.7 6.5 %collective-permute-start.12 = (bf16[1,34,256]{2,0,1:T(2,128)(2,1)S(1)}, bf16[1,34,256]{2,0,1:T(2,128)(2,1)S(1)}, u32[]{:S(2)}, u32[]{:S(2)}) collective-permute-start(bf16[1,34,256]{2,0,1:T(2,128)(2,1)S(1)} %get-tuple-element.51), channel_id=1, source_target_pairs={{0,4},{4,8},{8,12},{12,16},{16,20},{20,24},{24,28},{1,5},{5,9},{9,... | collective-permute-start | bytes 52232 | tf_op jit(solution)/shard_map/ppermute | solution.py:41
  97.0 5.7 %collective-permute-start.13 = (bf16[1,34,256]{2,0,1:T(2,128)(2,1)S(1)}, bf16[1,34,256]{2,0,1:T(2,128)(2,1)S(1)}, u32[]{:S(2)}, u32[]{:S(2)}) collective-permute-start(bf16[1,34,256]{2,0,1:T(2,128)(2,1)S(1)} %get-tuple-element.52), channel_id=1, source_target_pairs={{4,0},{8,4},{12,8},{16,12},{20,16},{24,20},{28,24},{5,1},{9,5},{13... | collective-permute-start | bytes 52232 | tf_op jit(solution)/shard_map/ppermute | solution.py:42
  98.3 11.5 %collective-permute-start.14 = (bf16[4,4,72,256]{3,2,1,0:T(8,128)(2,1)S(1)}, bf16[4,4,72,256]{3,2,1,0:T(8,128)(2,1)S(1)}, u32[]{:S(2)}, u32[]{:S(2)}) collective-permute-start(bf16[4,4,72,256]{3,2,1,0:T(8,128)(2,1)S(1)} %dynamic-slice_bitcast_fusion.1), channel_id=1, source_target_pairs={{0,4},{4,0},{8,12},{12,8},{16,20},{20,16},{24,28},{28,24},{1,5},{5... | collective-permute-start | bytes 1769480 | tf_op jit(solution)/shard_map/ppermute | solution.py:52
  103.0 0.7 copy-start.18
  105.7 6.5 %collective-permute-start.29 = (bf16[4,72,256]{2,1,0:T(8,128)(2,1)S(1)}, bf16[4,72,256]{2,1,0:T(8,128)(2,1)S(1)}, u32[]{:S(2)}, u32[]{:S(2)}) collective-permute-start(bf16[4,72,256]{2,1,0:T(8,128)(2,1)S(1)} %get-tuple-element.41), channel_id=1, source_target_pairs={{0,8},{4,12},{8,0},{12,4},{16,24},{20,28},{24,16},{28,20},{1,9},{5... | collective-permute-start | bytes 442376 | tf_op jit(solution)/shard_map/ppermute | solution.py:52
  108.3 9.5 %collective-permute-start.30 = (bf16[4,72,256]{2,1,0:T(8,128)(2,1)S(1)}, bf16[4,72,256]{2,1,0:T(8,128)(2,1)S(1)}, u32[]{:S(2)}, u32[]{:S(2)}) collective-permute-start(bf16[4,72,256]{2,1,0:T(8,128)(2,1)S(1)} %get-tuple-element.43), channel_id=1, source_target_pairs={{0,16},{4,20},{8,24},{12,28},{16,0},{20,4},{24,8},{28,12},{1,17},{... | collective-permute-start | bytes 442376 | tf_op jit(solution)/shard_map/ppermute | solution.py:52
  108.4 9.4 %collective-permute-start.31 = (bf16[4,72,256]{2,1,0:T(8,128)(2,1)S(1)}, bf16[4,72,256]{2,1,0:T(8,128)(2,1)S(1)}, u32[]{:S(2)}, u32[]{:S(2)}) collective-permute-start(bf16[4,72,256]{2,1,0:T(8,128)(2,1)S(1)} %get-tuple-element.42), channel_id=1, source_target_pairs={{0,24},{4,28},{8,16},{12,20},{16,8},{20,12},{24,0},{28,4},{1,25},{... | collective-permute-start | bytes 442376 | tf_op jit(solution)/shard_map/ppermute | solution.py:52
  110.1 11.8 %collective-permute-start.15 = (bf16[4,72,256]{2,1,0:T(8,128)(2,1)S(1)}, bf16[4,72,256]{2,1,0:T(8,128)(2,1)S(1)}, u32[]{:S(2)}, u32[]{:S(2)}) collective-permute-start(bf16[4,72,256]{2,1,0:T(8,128)(2,1)S(1)} %get-tuple-element.44), channel_id=1, source_target_pairs={{0,8},{4,12},{8,0},{12,4},{16,24},{20,28},{24,16},{28,20},{1,9},{5... | collective-permute-start | bytes 442376 | tf_op jit(solution)/shard_map/ppermute | solution.py:52
  112.1 12.1 %collective-permute-start.16 = (bf16[4,72,256]{2,1,0:T(8,128)(2,1)S(1)}, bf16[4,72,256]{2,1,0:T(8,128)(2,1)S(1)}, u32[]{:S(2)}, u32[]{:S(2)}) collective-permute-start(bf16[4,72,256]{2,1,0:T(8,128)(2,1)S(1)} %get-tuple-element.46), channel_id=1, source_target_pairs={{0,16},{4,20},{8,24},{12,28},{16,0},{20,4},{24,8},{28,12},{1,17},{... | collective-permute-start | bytes 442376 | tf_op jit(solution)/shard_map/ppermute | solution.py:52
  112.2 12.0 %collective-permute-start.17 = (bf16[4,72,256]{2,1,0:T(8,128)(2,1)S(1)}, bf16[4,72,256]{2,1,0:T(8,128)(2,1)S(1)}, u32[]{:S(2)}, u32[]{:S(2)}) collective-permute-start(bf16[4,72,256]{2,1,0:T(8,128)(2,1)S(1)} %get-tuple-element.45), channel_id=1, source_target_pairs={{0,24},{4,28},{8,16},{12,20},{16,8},{20,12},{24,0},{28,4},{1,25},{... | collective-permute-start | bytes 442376 | tf_op jit(solution)/shard_map/ppermute | solution.py:52
  118.0 10.3 %collective-permute-start.32 = (bf16[72,256]{1,0:T(8,128)(2,1)S(1)}, bf16[72,256]{1,0:T(8,128)(2,1)S(1)}, u32[]{:S(2)}, u32[]{:S(2)}) collective-permute-start(bf16[72,256]{1,0:T(8,128)(2,1)S(1)} %get-tuple-element.57), channel_id=1, source_target_pairs={{0,1},{1,0},{2,3},{3,2},{4,5},{5,4},{6,7},{7,6},{8,9},{9,8},{10,11... | collective-permute-start | bytes 110600 | tf_op jit(solution)/shard_map/ppermute | solution.py:52
  120.4 9.2 %collective-permute-start.33 = (bf16[72,256]{1,0:T(8,128)(2,1)S(1)}, bf16[72,256]{1,0:T(8,128)(2,1)S(1)}, u32[]{:S(2)}, u32[]{:S(2)}) collective-permute-start(bf16[72,256]{1,0:T(8,128)(2,1)S(1)} %get-tuple-element.59), channel_id=1, source_target_pairs={{0,2},{1,3},{2,0},{3,1},{4,6},{5,7},{6,4},{7,5},{8,10},{9,11},{10,... | collective-permute-start | bytes 110600 | tf_op jit(solution)/shard_map/ppermute | solution.py:52
  122.0 7.7 %collective-permute-start.34 = (bf16[72,256]{1,0:T(8,128)(2,1)S(1)}, bf16[72,256]{1,0:T(8,128)(2,1)S(1)}, u32[]{:S(2)}, u32[]{:S(2)}) collective-permute-start(bf16[72,256]{1,0:T(8,128)(2,1)S(1)} %get-tuple-element.58), channel_id=1, source_target_pairs={{0,3},{1,2},{2,1},{3,0},{4,7},{5,6},{6,5},{7,4},{8,11},{9,10},{10,... | collective-permute-start | bytes 110600 | tf_op jit(solution)/shard_map/ppermute | solution.py:52
  124.3 8.5 %collective-permute-start.18 = (bf16[72,256]{1,0:T(8,128)(2,1)S(1)}, bf16[72,256]{1,0:T(8,128)(2,1)S(1)}, u32[]{:S(2)}, u32[]{:S(2)}) collective-permute-start(bf16[72,256]{1,0:T(8,128)(2,1)S(1)} %get-tuple-element.60), channel_id=1, source_target_pairs={{0,1},{1,0},{2,3},{3,2},{4,5},{5,4},{6,7},{7,6},{8,9},{9,8},{10,11... | collective-permute-start | bytes 110600 | tf_op jit(solution)/shard_map/ppermute | solution.py:52
  126.7 7.4 %collective-permute-start.19 = (bf16[72,256]{1,0:T(8,128)(2,1)S(1)}, bf16[72,256]{1,0:T(8,128)(2,1)S(1)}, u32[]{:S(2)}, u32[]{:S(2)}) collective-permute-start(bf16[72,256]{1,0:T(8,128)(2,1)S(1)} %get-tuple-element.62), channel_id=1, source_target_pairs={{0,2},{1,3},{2,0},{3,1},{4,6},{5,7},{6,4},{7,5},{8,10},{9,11},{10,... | collective-permute-start | bytes 110600 | tf_op jit(solution)/shard_map/ppermute | solution.py:52
  128.3 5.9 %collective-permute-start.20 = (bf16[72,256]{1,0:T(8,128)(2,1)S(1)}, bf16[72,256]{1,0:T(8,128)(2,1)S(1)}, u32[]{:S(2)}, u32[]{:S(2)}) collective-permute-start(bf16[72,256]{1,0:T(8,128)(2,1)S(1)} %get-tuple-element.61), channel_id=1, source_target_pairs={{0,3},{1,2},{2,1},{3,0},{4,7},{5,6},{6,5},{7,4},{8,11},{9,10},{10,... | collective-permute-start | bytes 110600 | tf_op jit(solution)/shard_map/ppermute | solution.py:52
  129.7 7.6 %collective-permute-start.35 = (bf16[72,256]{1,0:T(8,128)(2,1)S(1)}, bf16[72,256]{1,0:T(8,128)(2,1)S(1)}, u32[]{:S(2)}, u32[]{:S(2)}) collective-permute-start(bf16[72,256]{1,0:T(8,128)(2,1)S(1)} %get-tuple-element.38), channel_id=1, source_target_pairs={{0,1},{1,0},{2,3},{3,2},{4,5},{5,4},{6,7},{7,6},{8,9},{9,8},{10,11... | collective-permute-start | bytes 110600 | tf_op jit(solution)/shard_map/ppermute | solution.py:52
  130.4 8.3 %collective-permute-start.36 = (bf16[72,256]{1,0:T(8,128)(2,1)S(1)}, bf16[72,256]{1,0:T(8,128)(2,1)S(1)}, u32[]{:S(2)}, u32[]{:S(2)}) collective-permute-start(bf16[72,256]{1,0:T(8,128)(2,1)S(1)} %get-tuple-element.38), channel_id=1, source_target_pairs={{0,2},{1,3},{2,0},{3,1},{4,6},{5,7},{6,4},{7,5},{8,10},{9,11},{10,... | collective-permute-start | bytes 110600 | tf_op jit(solution)/shard_map/ppermute | solution.py:52
  132.8 5.9 %collective-permute-start.37 = (bf16[72,256]{1,0:T(8,128)(2,1)S(1)}, bf16[72,256]{1,0:T(8,128)(2,1)S(1)}, u32[]{:S(2)}, u32[]{:S(2)}) collective-permute-start(bf16[72,256]{1,0:T(8,128)(2,1)S(1)} %get-tuple-element.38), channel_id=1, source_target_pairs={{0,3},{1,2},{2,1},{3,0},{4,7},{5,6},{6,5},{7,4},{8,11},{9,10},{10,... | collective-permute-start | bytes 110600 | tf_op jit(solution)/shard_map/ppermute | solution.py:52
  134.2 5.9 %collective-permute-start.21 = (bf16[72,256]{1,0:T(8,128)(2,1)S(1)}, bf16[72,256]{1,0:T(8,128)(2,1)S(1)}, u32[]{:S(2)}, u32[]{:S(2)}) collective-permute-start(bf16[72,256]{1,0:T(8,128)(2,1)S(1)} %get-tuple-element.40), channel_id=1, source_target_pairs={{0,1},{1,0},{2,3},{3,2},{4,5},{5,4},{6,7},{7,6},{8,9},{9,8},{10,11... | collective-permute-start | bytes 110600 | tf_op jit(solution)/shard_map/ppermute | solution.py:52
  135.5 6.8 %collective-permute-start.22 = (bf16[72,256]{1,0:T(8,128)(2,1)S(1)}, bf16[72,256]{1,0:T(8,128)(2,1)S(1)}, u32[]{:S(2)}, u32[]{:S(2)}) collective-permute-start(bf16[72,256]{1,0:T(8,128)(2,1)S(1)} %get-tuple-element.40), channel_id=1, source_target_pairs={{0,2},{1,3},{2,0},{3,1},{4,6},{5,7},{6,4},{7,5},{8,10},{9,11},{10,... | collective-permute-start | bytes 110600 | tf_op jit(solution)/shard_map/ppermute | solution.py:52
  137.3 5.8 %collective-permute-start.23 = (bf16[72,256]{1,0:T(8,128)(2,1)S(1)}, bf16[72,256]{1,0:T(8,128)(2,1)S(1)}, u32[]{:S(2)}, u32[]{:S(2)}) collective-permute-start(bf16[72,256]{1,0:T(8,128)(2,1)S(1)} %get-tuple-element.40), channel_id=1, source_target_pairs={{0,3},{1,2},{2,1},{3,0},{4,7},{5,6},{6,5},{7,4},{8,11},{9,10},{10,... | collective-permute-start | bytes 110600 | tf_op jit(solution)/shard_map/ppermute | solution.py:52
  138.8 6.6 %collective-permute-start.38 = (bf16[4,72,256]{2,1,0:T(8,128)(2,1)S(1)}, bf16[4,72,256]{2,1,0:T(8,128)(2,1)S(1)}, u32[]{:S(2)}, u32[]{:S(2)}) collective-permute-start(bf16[4,72,256]{2,1,0:T(8,128)(2,1)S(1)} %bitcast_dynamic-update-slice_fusion.12), channel_id=1, source_target_pairs={{0,8},{4,12},{8,0},{12,4},{16,24},{20,28},{24,16},{28,20},{1,9},{5... | collective-permute-start | bytes 442376 | tf_op jit(solution)/shard_map/ppermute | solution.py:52
  138.8 8.0 %collective-permute-start.39 = (bf16[4,72,256]{2,1,0:T(8,128)(2,1)S(1)}, bf16[4,72,256]{2,1,0:T(8,128)(2,1)S(1)}, u32[]{:S(2)}, u32[]{:S(2)}) collective-permute-start(bf16[4,72,256]{2,1,0:T(8,128)(2,1)S(1)} %bitcast_dynamic-update-slice_fusion.12), channel_id=1, source_target_pairs={{0,16},{4,20},{8,24},{12,28},{16,0},{20,4},{24,8},{28,12},{1,17},{... | collective-permute-start | bytes 442376 | tf_op jit(solution)/shard_map/ppermute | solution.py:52
  140.1 8.3 %collective-permute-start.40 = (bf16[4,72,256]{2,1,0:T(8,128)(2,1)S(1)}, bf16[4,72,256]{2,1,0:T(8,128)(2,1)S(1)}, u32[]{:S(2)}, u32[]{:S(2)}) collective-permute-start(bf16[4,72,256]{2,1,0:T(8,128)(2,1)S(1)} %bitcast_dynamic-update-slice_fusion.12), channel_id=1, source_target_pairs={{0,24},{4,28},{8,16},{12,20},{16,8},{20,12},{24,0},{28,4},{1,25},{... | collective-permute-start | bytes 442376 | tf_op jit(solution)/shard_map/ppermute | solution.py:52
  143.1 7.4 %collective-permute-start.24 = (bf16[4,72,256]{2,1,0:T(8,128)(2,1)S(1)}, bf16[4,72,256]{2,1,0:T(8,128)(2,1)S(1)}, u32[]{:S(2)}, u32[]{:S(2)}) collective-permute-start(bf16[4,72,256]{2,1,0:T(8,128)(2,1)S(1)} %bitcast_dynamic-update-slice_fusion.16), channel_id=1, source_target_pairs={{0,8},{4,12},{8,0},{12,4},{16,24},{20,28},{24,16},{28,20},{1,9},{5... | collective-permute-start | bytes 442376 | tf_op jit(solution)/shard_map/ppermute | solution.py:52
  143.1 9.4 %collective-permute-start.25 = (bf16[4,72,256]{2,1,0:T(8,128)(2,1)S(1)}, bf16[4,72,256]{2,1,0:T(8,128)(2,1)S(1)}, u32[]{:S(2)}, u32[]{:S(2)}) collective-permute-start(bf16[4,72,256]{2,1,0:T(8,128)(2,1)S(1)} %bitcast_dynamic-update-slice_fusion.16), channel_id=1, source_target_pairs={{0,16},{4,20},{8,24},{12,28},{16,0},{20,4},{24,8},{28,12},{1,17},{... | collective-permute-start | bytes 442376 | tf_op jit(solution)/shard_map/ppermute | solution.py:52
  145.3 7.2 %collective-permute-start.26 = (bf16[4,72,256]{2,1,0:T(8,128)(2,1)S(1)}, bf16[4,72,256]{2,1,0:T(8,128)(2,1)S(1)}, u32[]{:S(2)}, u32[]{:S(2)}) collective-permute-start(bf16[4,72,256]{2,1,0:T(8,128)(2,1)S(1)} %bitcast_dynamic-update-slice_fusion.16), channel_id=1, source_target_pairs={{0,24},{4,28},{8,16},{12,20},{16,8},{20,12},{24,0},{28,4},{1,25},{... | collective-permute-start | bytes 442376 | tf_op jit(solution)/shard_map/ppermute | solution.py:52
  148.4 4.5 %collective-permute-start.41 = (bf16[4,4,72,256]{3,2,1,0:T(8,128)(2,1)S(1)}, bf16[4,4,72,256]{3,2,1,0:T(8,128)(2,1)S(1)}, u32[]{:S(2)}, u32[]{:S(2)}) collective-permute-start(bf16[4,4,72,256]{3,2,1,0:T(8,128)(2,1)S(1)} %bitcast_dynamic-update-slice_fusion.4), channel_id=1, source_target_pairs={{0,4},{4,0},{8,12},{12,8},{16,20},{20,16},{24,28},{28,24},{1,5},{5... | collective-permute-start | bytes 1769480 | tf_op jit(solution)/shard_map/ppermute | solution.py:52
  152.5 2.1 %collective-permute-start.27 = (bf16[4,4,72,256]{3,2,1,0:T(8,128)(2,1)S(1)}, bf16[4,4,72,256]{3,2,1,0:T(8,128)(2,1)S(1)}, u32[]{:S(2)}, u32[]{:S(2)}) collective-permute-start(bf16[4,4,72,256]{3,2,1,0:T(8,128)(2,1)S(1)} %bitcast_dynamic-update-slice_fusion.8), channel_id=1, source_target_pairs={{0,4},{4,0},{8,12},{12,8},{16,20},{20,16},{24,28},{28,24},{1,5},{5... | collective-permute-start | bytes 1769480 | tf_op jit(solution)/shard_map/ppermute | solution.py:52
